TPU v7x, 512 devices: a whole 4x4x16 slice. The times are simulated.
512 devices in a mesh: view: 8 (over y, core), scene: 64 (over x, z).
Axes of the slice: x: 4, y: 4, z: 16, core: 2. Of those that a mesh axis runs over, the one named last changes fastest.
Arguments:
- means: float32 [1024, 3, 128], P(('view', 'scene')), may hold values from -3 to 3
- log_scales: float32 [1024, 3, 128], P(('view', 'scene')), may hold values from -3.3 to -0.4, as said below
- rotations: float32 [1024, 4, 128], P(('view', 'scene')), may hold values from -2.5 to 2.5
- opacity_logits: float32 [1024, 1, 128], P(('view', 'scene')), may hold values from -3 to 3
- colour_coefs: float32 [1024, 48, 128], P(('view', 'scene')), may hold values from -2 to 2
- cameras: float32 [8, 16], replicated, may hold values from -1 to 2048, as said below
- exposure: float32 [8, 12], P('view'), may hold values from -1 to 1
- target: float32 [8, 1024, 3, 256], P('view', 'scene'), may hold values from 0 to 1
- tile_ids: int32 [8, 1024], P('view', 'scene'), may hold values from 0 to 1023, each once within a row
- send_list: int32 [8, 64, 64, 2], P('view', 'scene'), may hold values from -1 to 15, as said below
- pair_slots: int32 [8, 1024, 4], P('view', 'scene'), may hold values from -1 to 127, as said below
Outputs:
- shown: float32 [8, 1024, 3, 256], P('view', 'scene')
- grad_means: float32 [1024, 3, 128], P(('view', 'scene'))
- grad_log_scales: float32 [1024, 3, 128], P(('view', 'scene'))
- grad_rotations: float32 [1024, 4, 128], P(('view', 'scene'))
- grad_opacity: float32 [1024, 1, 128], P(('view', 'scene'))
- grad_colour: float32 [1024, 48, 128], P(('view', 'scene'))
- grad_exposure: float32 [8, 12], P('view')
Inputs may be any that keep to these rules, and one draw needn't show every extreme that they name: send_list[v, s, r, c] is a local block number of owner s or -1; in each row of 2 the live entries come first and are all different, and a row may have none; in every image some renderer gets 2 blocks from every owner. pair_slots[v, t, k] is -1 or s * 2 + c with c below the number of live entries of send_list[v, s, t // 16]; a tile's live entries come first, at least one, all different; in every image each renderer has a tile with 4 live entries. `cameras`: each row is a rotation matrix, a translation, two focal lengths and a principal point; every Gaussian lies at depth 4 or more before each camera. `log_scales`: logarithms of lengths in world units.
All inputs are finite; a program needn't handle non-finite values.
Results may differ from a plain program's by a relative error of at most 0.0003.
Values sent between devices are 32-bit elements; how exact they have to be, the bound alone decides.
No kernel may reach another device: no remote copies, remote signals or barrier semaphores. Data moves between devices by JAX's collectives and lax.ppermute only.
A program may use at most 64 MiB of HBM per device.

v0:
```python
import jax
import jax.numpy as jnp
from jax import lax
from jax.sharding import PartitionSpec as P

PIX = 256
TILE_COLS = 32


SH_ZERO = 0.28209479177387814
SH_ONE = 0.4886025119029199
SH_TWO = (
    1.0925484305920792,
    -1.0925484305920792,
    0.31539156525252005,
    -1.0925484305920792,
    0.5462742152960396,
)
SH_THREE = (
    -0.5900435899266435,
    2.890611442640554,
    -0.4570457994644658,
    0.3731763325901154,
    -0.4570457994644658,
    1.445305721320277,
    -0.5900435899266435,
)


def sent_to_all(shard, axis):
    copies = jnp.broadcast_to(shard, (lax.axis_size(axis), *shard.shape))
    return lax.all_to_all(copies, axis, split_axis=0, concat_axis=0, tiled=True)


def of_everyone(shard, axis):
    everything = sent_to_all(shard, axis)
    return jnp.sum(everything, axis=0)


def harmonics(dir_x, dir_y, dir_z):
    sq_x, sq_y, sq_z = (dir_x * dir_x, dir_y * dir_y, dir_z * dir_z)
    sh_basis = [
        SH_ZERO * jnp.ones_like(dir_x),
        -SH_ONE * dir_y,
        SH_ONE * dir_z,
        -SH_ONE * dir_x,
        SH_TWO[0] * dir_x * dir_y,
        SH_TWO[1] * dir_y * dir_z,
        SH_TWO[2] * (2.0 * sq_z - sq_x - sq_y),
        SH_TWO[3] * dir_x * dir_z,
        SH_TWO[4] * (sq_x - sq_y),
        SH_THREE[0] * dir_y * (3.0 * sq_x - sq_y),
        SH_THREE[1] * dir_x * dir_y * dir_z,
        SH_THREE[2] * dir_y * (4.0 * sq_z - sq_x - sq_y),
        SH_THREE[3] * dir_z * (2.0 * sq_z - 3.0 * sq_x - 3.0 * sq_y),
        SH_THREE[4] * dir_x * (4.0 * sq_z - sq_x - sq_y),
        SH_THREE[5] * dir_z * (sq_x - sq_y),
        SH_THREE[6] * dir_x * (sq_x - 3.0 * sq_y),
    ]
    return jnp.stack(sh_basis, axis=1)


def project(pieces, camera):
    means, log_scales, rotations, opacity_logits, colour_coefs = pieces
    rotation = camera[0:9].reshape(3, 3)
    translation = camera[9:12]
    focal_x, focal_y, centre_x, centre_y = (camera[12], camera[13], camera[14], camera[15])
    position = [means[:, 0], means[:, 1], means[:, 2]]
    view_pos = [
        rotation[row_at, 0] * position[0]
        + rotation[row_at, 1] * position[1]
        + rotation[row_at, 2] * position[2]
        + translation[row_at]
        for row_at in range(3)
    ]
    inv_depth = 1.0 / view_pos[2]
    quat_w = rotations[:, 0] + 3.0
    quat_x, quat_y, quat_z = (rotations[:, 1], rotations[:, 2], rotations[:, 3])
    quat_norm = jnp.sqrt(quat_w * quat_w + quat_x * quat_x + quat_y * quat_y + quat_z * quat_z)
    quat_w, quat_x, quat_y, quat_z = (
        quat_w / quat_norm,
        quat_x / quat_norm,
        quat_y / quat_norm,
        quat_z / quat_norm,
    )
    spin_matrix = [
        [
            1.0 - 2.0 * (quat_y * quat_y + quat_z * quat_z),
            2.0 * (quat_x * quat_y - quat_w * quat_z),
            2.0 * (quat_x * quat_z + quat_w * quat_y),
        ],
        [
            2.0 * (quat_x * quat_y + quat_w * quat_z),
            1.0 - 2.0 * (quat_x * quat_x + quat_z * quat_z),
            2.0 * (quat_y * quat_z - quat_w * quat_x),
        ],
        [
            2.0 * (quat_x * quat_z - quat_w * quat_y),
            2.0 * (quat_y * quat_z + quat_w * quat_x),
            1.0 - 2.0 * (quat_x * quat_x + quat_y * quat_y),
        ],
    ]
    scales = jnp.exp(log_scales)
    world_frame = [
        [spin_matrix[row_at][col_at] * scales[:, col_at] for col_at in range(3)]
        for row_at in range(3)
    ]
    jacobian = [
        [
            focal_x * inv_depth * rotation[0, col_at]
            - focal_x * view_pos[0] * inv_depth * inv_depth * rotation[2, col_at]
            for col_at in range(3)
        ],
        [
            focal_y * inv_depth * rotation[1, col_at]
            - focal_y * view_pos[1] * inv_depth * inv_depth * rotation[2, col_at]
            for col_at in range(3)
        ],
    ]
    screen_frame = [
        [
            jacobian[row_at][0] * world_frame[0][col_at]
            + jacobian[row_at][1] * world_frame[1][col_at]
            + jacobian[row_at][2] * world_frame[2][col_at]
            for col_at in range(3)
        ]
        for row_at in range(2)
    ]
    sigma_xx = screen_frame[0][0] ** 2 + screen_frame[0][1] ** 2 + screen_frame[0][2] ** 2 + 0.3
    sigma_yy = screen_frame[1][0] ** 2 + screen_frame[1][1] ** 2 + screen_frame[1][2] ** 2 + 0.3
    sigma_xy = (
        screen_frame[0][0] * screen_frame[1][0]
        + screen_frame[0][1] * screen_frame[1][1]
        + screen_frame[0][2] * screen_frame[1][2]
    )
    determinant = sigma_xx * sigma_yy - sigma_xy * sigma_xy
    screen_x = focal_x * view_pos[0] * inv_depth + centre_x
    screen_y = focal_y * view_pos[1] * inv_depth + centre_y
    opacity = jax.nn.sigmoid(opacity_logits[:, 0])
    eye_pos = [
        -(
            rotation[0, col_at] * translation[0]
            + rotation[1, col_at] * translation[1]
            + rotation[2, col_at] * translation[2]
        )
        for col_at in range(3)
    ]
    offsets = [position[col_at] - eye_pos[col_at] for col_at in range(3)]
    eye_dist = jnp.sqrt(offsets[0] ** 2 + offsets[1] ** 2 + offsets[2] ** 2)
    sh_basis = harmonics(offsets[0] / eye_dist, offsets[1] / eye_dist, offsets[2] / eye_dist)
    sh_coefs = colour_coefs.reshape(colour_coefs.shape[0], 16, 3, colour_coefs.shape[2])
    colour = jnp.maximum(0.5 + jnp.sum(sh_basis[:, :, None, :] * sh_coefs, axis=1), 0.0)
    shape_rows = jnp.stack(
        [
            screen_x,
            screen_y,
            sigma_yy / determinant,
            -sigma_xy / determinant,
            sigma_xx / determinant,
            opacity,
        ],
        axis=1,
    )
    return jnp.concatenate([shape_rows, colour], axis=1)


def composite(chosen_blk, live_mask, tile_id):
    lane_count = chosen_blk.shape[2]
    pixel_index = jnp.arange(PIX, dtype=jnp.int32)
    pixel_x = (16 * (tile_id % TILE_COLS) + pixel_index % 16).astype(jnp.float32) + 0.5
    pixel_y = (16 * (tile_id // TILE_COLS) + pixel_index // 16).astype(jnp.float32) + 0.5
    gap_x = pixel_x[None, :, None] - chosen_blk[:, 0][:, None, :]
    gap_y = pixel_y[None, :, None] - chosen_blk[:, 1][:, None, :]
    falloff = (
        0.5
        * (
            chosen_blk[:, 2][:, None, :] * gap_x * gap_x
            + chosen_blk[:, 4][:, None, :] * gap_y * gap_y
        )
        + chosen_blk[:, 3][:, None, :] * gap_x * gap_y
    )
    alpha_vals = (
        chosen_blk[:, 5][:, None, :]
        * jnp.exp(-falloff)
        * live_mask.astype(jnp.float32)[:, None, None]
    )
    log_keep = jnp.log1p(-alpha_vals)
    lane_index = jnp.arange(lane_count)
    strict = (lane_index[:, None] < lane_index[None, :]).astype(jnp.float32)
    inside = jnp.dot(
        log_keep.reshape(-1, lane_count), strict, precision=lax.Precision.HIGHEST
    ).reshape(log_keep.shape)
    totals = jnp.sum(log_keep, axis=2)
    before = jnp.cumsum(totals, axis=0) - totals
    transmit = jnp.exp(inside + before[:, :, None])
    return jnp.einsum(
        "kpg,kcg->cp", alpha_vals * transmit, chosen_blk[:, 6:9], precision=lax.Precision.HIGHEST
    )


def local(
    means,
    log_scales,
    rotations,
    opacity_logits,
    colour_coefs,
    cameras,
    exposure,
    target,
    tile_ids,
    send_list,
    pair_slots,
):
    view_count = lax.axis_size("view")
    scene_count = lax.axis_size("scene")
    own_params = (means, log_scales, rotations, opacity_logits, colour_coefs)
    per_device = means.shape[0]
    owned_count = per_device * view_count
    feature_count = 9
    lane_count = means.shape[2]
    capacity = send_list.shape[3]
    own_proj, unproject = jax.vjp(
        lambda *pieces: jax.vmap(lambda cam_row: project(pieces, cam_row))(cameras), *own_params
    )
    arrived = lax.all_to_all(own_proj, "view", split_axis=0, concat_axis=0, tiled=True)
    projected = arrived.reshape(owned_count, feature_count, lane_count)
    send_picks = send_list[0, 0]
    outgoing = jnp.take(projected, jnp.maximum(send_picks, 0).reshape(-1), axis=0)
    outgoing = (
        outgoing.reshape(scene_count, capacity, feature_count, lane_count)
        * (send_picks >= 0).astype(jnp.float32)[:, :, None, None]
    )
    incoming = lax.all_to_all(outgoing, "scene", split_axis=0, concat_axis=0, tiled=True).reshape(
        scene_count * capacity, feature_count, lane_count
    )
    mixing = jnp.eye(3, dtype=jnp.float32) + exposure[0, 0:9].reshape(3, 3)
    offset = exposure[0, 9:12]

    def render_tile(tile_items):
        tile_id, slot_list, goal_tile = tile_items
        live_mask = slot_list >= 0
        chosen = jnp.take(incoming, jnp.maximum(slot_list, 0), axis=0)
        colour, shade_back = jax.vjp(
            lambda chosen_blk: composite(chosen_blk, live_mask, tile_id), chosen
        )
        shown_tile = jnp.dot(mixing, colour, precision=lax.Precision.HIGHEST) + offset[:, None]
        miss_tile = shown_tile - goal_tile
        grad_chosen = shade_back(jnp.dot(mixing.T, miss_tile, precision=lax.Precision.HIGHEST))[0]
        expo_terms = jnp.concatenate(
            [
                jnp.dot(miss_tile, colour.T, precision=lax.Precision.HIGHEST).reshape(9),
                jnp.sum(miss_tile, axis=1),
            ]
        )
        return (shown_tile, grad_chosen, expo_terms)

    shown_tiles, grad_chosen, expo_terms = lax.map(
        render_tile, (tile_ids[0], pair_slots[0], target[0])
    )
    dump_index = scene_count * capacity
    where_to = jnp.where(pair_slots[0] >= 0, pair_slots[0], dump_index).reshape(-1)
    grad_incoming = (
        jnp.zeros((dump_index, feature_count, lane_count), jnp.float32)
        .at[where_to]
        .add(grad_chosen.reshape(-1, feature_count, lane_count), mode="drop")
    )
    returned = lax.all_to_all(
        grad_incoming.reshape(scene_count, capacity, feature_count, lane_count),
        "scene",
        split_axis=0,
        concat_axis=0,
        tiled=True,
    )
    home_index = jnp.where(send_picks >= 0, send_picks, owned_count).reshape(-1)
    grad_projected = (
        jnp.zeros((owned_count, feature_count, lane_count), jnp.float32)
        .at[home_index]
        .add(returned.reshape(-1, feature_count, lane_count), mode="drop")
    )
    sent_back = lax.all_to_all(
        grad_projected.reshape(view_count, per_device, feature_count, lane_count),
        "view",
        split_axis=0,
        concat_axis=0,
        tiled=True,
    )
    param_grads = unproject(sent_back)
    exposure_grad = of_everyone(jnp.sum(expo_terms, axis=0), "scene")
    return (
        shown_tiles[None],
        param_grads[0],
        param_grads[1],
        param_grads[2],
        param_grads[3],
        param_grads[4],
        exposure_grad[None],
    )


def solution(mesh):
    return jax.shard_map(
        local,
        mesh=mesh,
        in_specs=(
            P(("view", "scene"), None, None),
            P(("view", "scene"), None, None),
            P(("view", "scene"), None, None),
            P(("view", "scene"), None, None),
            P(("view", "scene"), None, None),
            P(),
            P("view", None),
            P("view", "scene", None, None),
            P("view", "scene"),
            P("view", "scene", None, None),
            P("view", "scene", None),
        ),
        out_specs=(
            P("view", "scene", None, None),
            P(("view", "scene"), None, None),
            P(("view", "scene"), None, None),
            P(("view", "scene"), None, None),
            P(("view", "scene"), None, None),
            P(("view", "scene"), None, None),
            P("view", None),
        ),
        check_vma=False,
    )
```

profile of v0, /device:TPU:1, one launch (start us, length us, event | category | flops | bytes accessed | tf_op | source)
XLA Modules:
  0.0 325.6 jit_solution(6508875844462213335)
XLA Ops:
  7.1 10.2 %all-to-all-start = ((f32[8,2,9,128]{3,1,2,0:T(2,128)}), f32[8,2,9,128]{3,1,2,0:T(2,128)S(1)}, u32[]{:S(2)}, u32[]{:S(2)}) async-start(f32[8,2,9,128]{3,1,2,0:T(2,128)} %copy.1068), calls=%async_computation | async-start | bytes 147456 | tf_op jit(solution)/shard_map/all_to_all | solution.py:225
  17.8 4.4 %all-to-all-done = f32[8,2,9,128]{3,1,2,0:T(2,128)S(1)} async-done(((f32[8,2,9,128]{3,1,2,0:T(2,128)}), f32[8,2,9,128]{3,1,2,0:T(2,128)S(1)}, u32[]{:S(2)}, u32[]{:S(2)}) %all-to-all-start) | async-done | bytes 73760 | tf_op jit(solution)/shard_map/all_to_all | solution.py:225
  24.2 14.3 %all-to-all-start.1 = ((f32[64,2,9,128]{3,1,2,0:T(2,128)}), f32[64,2,9,128]{3,1,2,0:T(2,128)S(1)}, u32[]{:S(2)}, u32[]{:S(2)}) async-start(f32[64,2,9,128]{3,1,2,0:T(2,128)} %fusion.49), calls=%async_computation.1 | async-start | bytes 1179648 | tf_op jit(solution)/shard_map/all_to_all | solution.py:233
  40.3 30.1 %all-to-all-done.1 = f32[64,2,9,128]{3,1,2,0:T(2,128)S(1)} async-done(((f32[64,2,9,128]{3,1,2,0:T(2,128)}), f32[64,2,9,128]{3,1,2,0:T(2,128)S(1)}, u32[]{:S(2)}, u32[]{:S(2)}) %all-to-all-start.1) | async-done | bytes 589856 | tf_op jit(solution)/shard_map/all_to_all | solution.py:233
  71.7 170.7 %while.17 = (s32[]{:T(128)}, f32[16,3,256]{2,0,1:T(8,128)S(1)}, f32[16,4,9,128]{3,2,1,0:T(8,128)S(1)}, f32[16,12]{1,0:T(8,128)S(1)}, s32[16,4]{1,0:T(8,128)S(1)}...) while((s32[]{:T(128)}, f32[16,3,256]{2,0,1:T(8,128)S(1)}, ...), condition=%wide.region_13.14_spmd, body=%wide.region_1.13_spmd.sunk | while | flops 435844416 | bytes 4063208 | solution.py:257
  90.2 1.7 fusion.234
  100.9 1.7 fusion.234
  111.5 1.7 fusion.234
  122.2 1.7 fusion.234
  132.9 1.7 fusion.234
  143.5 1.7 fusion.234
  154.2 1.7 fusion.234
  164.9 1.7 fusion.234
  175.5 1.7 fusion.234
  186.2 1.7 fusion.234
  196.9 1.7 fusion.234
  243.0 2.9 scatter_fusion
  247.0 8.9 %all-to-all-start.2 = ((f32[64,2,9,128]{3,1,2,0:T(2,128)}), f32[64,2,9,128]{3,1,2,0:T(2,128)S(1)}, u32[]{:S(2)}, u32[]{:S(2)}) async-start(f32[64,2,9,128]{3,1,2,0:T(2,128)} %copy.1079), calls=%async_computation.2 | async-start | bytes 1179648 | tf_op jit(solution)/shard_map/all_to_all | solution.py:267
  256.0 31.9 %all-to-all-done.2 = f32[64,2,9,128]{3,1,2,0:T(2,128)S(1)} async-done(((f32[64,2,9,128]{3,1,2,0:T(2,128)}), f32[64,2,9,128]{3,1,2,0:T(2,128)S(1)}, u32[]{:S(2)}, u32[]{:S(2)}) %all-to-all-start.2) | async-done | bytes 589856 | tf_op jit(solution)/shard_map/all_to_all | solution.py:267
  288.6 9.0 %all-to-all-start.4 = ((f32[64,1,12]{2,1,0:T(1,128)}), f32[64,1,12]{2,1,0:T(1,128)S(1)}, u32[]{:S(2)}, u32[]{:S(2)}) async-start(f32[64,1,12]{2,1,0:T(1,128)} %broadcast_in_dim.187), calls=%async_computation.4 | async-start | bytes 65536 | tf_op jit(solution)/shard_map/all_to_all | solution.py:32
  298.2 5.4 %scatter_fusion.1 = f32[16,9,128]{2,1,0:T(8,128)S(1)} fusion(f32[16,9,128]{2,1,0:T(8,128)S(1)} %broadcast_in_dim.181, s32[128]{0:T(128)S(1)} %get-tuple-element.541, f32[128,9,128]{2,1,0:T(8,128)S(1)} %copy.1081), kind=kCustom, calls=%fused_computation.3 | custom fusion | flops 147456 | bytes 1769984 | tf_op jit(solution)/shard_map/scatter-add | solution.py:278
  304.3 6.4 %all-to-all-done.4 = f32[64,1,12]{2,1,0:T(1,128)S(1)} async-done(((f32[64,1,12]{2,1,0:T(1,128)}), f32[64,1,12]{2,1,0:T(1,128)S(1)}, u32[]{:S(2)}, u32[]{:S(2)}) %all-to-all-start.4) | async-done | bytes 3104 | tf_op jit(solution)/shard_map/all_to_all | solution.py:32
  310.6 5.6 %all-to-all-start.3 = ((f32[8,2,9,128]{3,1,2,0:T(2,128)}), f32[8,2,9,128]{3,1,2,0:T(2,128)S(1)}, u32[]{:S(2)}, u32[]{:S(2)}) async-start(f32[8,2,9,128]{3,1,2,0:T(2,128)} %copy.1082), calls=%async_computation.3 | async-start | bytes 147456 | tf_op jit(solution)/shard_map/all_to_all | solution.py:280
  316.8 4.3 %all-to-all-done.3 = f32[8,2,9,128]{3,1,2,0:T(2,128)S(1)} async-done(((f32[8,2,9,128]{3,1,2,0:T(2,128)}), f32[8,2,9,128]{3,1,2,0:T(2,128)S(1)}, u32[]{:S(2)}, u32[]{:S(2)}) %all-to-all-start.3) | async-done | bytes 73760 | tf_op jit(solution)/shard_map/all_to_all | solution.py:280
  (587 shorter events, 128.3 us)
Async XLA Ops:
  0.6 0.7 copy-start
  1.3 0.7 copy-start.8
  3.6 0.7 copy-start.4
  4.3 0.7 copy-start.3
  5.2 0.8 copy-start.2
  5.3 0.7 copy-start.7
  7.1 10.2 %copy-start.6 = (s32[1,1,64,2]{2,3,1,0:T(2,128)S(1)}, s32[1,1,64,2]{2,3,1,0:T(2,128)}, u32[]{:S(2)}) copy-start(s32[1,1,64,2]{2,3,1,0:T(2,128)} %param.22) | copy-start | bytes 1540
  7.1 15.1 %all-to-all-start = ((f32[8,2,9,128]{3,1,2,0:T(2,128)}), f32[8,2,9,128]{3,1,2,0:T(2,128)S(1)}, u32[]{:S(2)}, u32[]{:S(2)}) async-start(f32[8,2,9,128]{3,1,2,0:T(2,128)} %copy.1068), calls=%async_computation | async-start | bytes 147456 | tf_op jit(solution)/shard_map/all_to_all | solution.py:225
  24.2 15.9 %copy-start.1 = (f32[1,16,3,256]{3,1,2,0:T(8,128)S(1)}, f32[1,16,3,256]{3,1,2,0:T(8,128)}, u32[]{:S(2)}) copy-start(f32[1,16,3,256]{3,1,2,0:T(8,128)} %param.20) | copy-start | bytes 147460
  24.2 46.2 %all-to-all-start.1 = ((f32[64,2,9,128]{3,1,2,0:T(2,128)}), f32[64,2,9,128]{3,1,2,0:T(2,128)S(1)}, u32[]{:S(2)}, u32[]{:S(2)}) async-start(f32[64,2,9,128]{3,1,2,0:T(2,128)} %fusion.49), calls=%async_computation.1 | async-start | bytes 1179648 | tf_op jit(solution)/shard_map/all_to_all | solution.py:233
  38.5 0.7 copy-start.5
  39.3 0.7 copy-start.10
  71.0 0.7 copy-start.11
  242.4 0.6 copy-start.9
  247.0 40.9 %all-to-all-start.2 = ((f32[64,2,9,128]{3,1,2,0:T(2,128)}), f32[64,2,9,128]{3,1,2,0:T(2,128)S(1)}, u32[]{:S(2)}, u32[]{:S(2)}) async-start(f32[64,2,9,128]{3,1,2,0:T(2,128)} %copy.1079), calls=%async_computation.2 | async-start | bytes 1179648 | tf_op jit(solution)/shard_map/all_to_all | solution.py:267
  288.6 22.0 %all-to-all-start.4 = ((f32[64,1,12]{2,1,0:T(1,128)}), f32[64,1,12]{2,1,0:T(1,128)S(1)}, u32[]{:S(2)}, u32[]{:S(2)}) async-start(f32[64,1,12]{2,1,0:T(1,128)} %broadcast_in_dim.187), calls=%async_computation.4 | async-start | bytes 65536 | tf_op jit(solution)/shard_map/all_to_all | solution.py:32
  310.6 10.5 %all-to-all-start.3 = ((f32[8,2,9,128]{3,1,2,0:T(2,128)}), f32[8,2,9,128]{3,1,2,0:T(2,128)S(1)}, u32[]{:S(2)}, u32[]{:S(2)}) async-start(f32[8,2,9,128]{3,1,2,0:T(2,128)} %copy.1082), calls=%async_computation.3 | async-start | bytes 147456 | tf_op jit(solution)/shard_map/all_to_all | solution.py:280
where the time goes:
time: 327 us; the launch traced here: 326 us
  matrix products  91 us (28%)
  waiting for transfers between devices  77.2 us (24%)
  starting transfers between devices  48 us (15%)
  loops' own time  43.7 us (13%)
  local copies, waits for them, and re-layouts  34.3 us (10%)
  other arithmetic  30.2 us (9%)
    another operation x1, loops' own time, local(): lax.map(render_tile, (tile_ids[0], pair_slots[0], target[0]))  43.7 us
    dot_general x32, matrix products, composite(): jnp.dot(log_keep.reshape(-1, lane_count), strict, precision=lax.Precision...  41.3 us
    dot_general x48, matrix products, composite(): jnp.einsum('kpg,kcg->cp', alpha_vals * transmit, chosen_blk[:, 6:9], prec...  40.5 us
    all_to_all x1, waiting for transfers between devices, local(): lax.all_to_all(grad_incoming.reshape(scene_count, capacity, feature_count...  31.9 us
    all_to_all x1, waiting for transfers between devices, local(): lax.all_to_all(outgoing, 'scene', split_axis=0, concat_axis=0, tiled=True)  30.1 us
    all_to_all x1, starting transfers between devices, local(): lax.all_to_all(outgoing, 'scene', split_axis=0, concat_axis=0, tiled=True)  14.3 us
    all_to_all x1, starting transfers between devices, local(): lax.all_to_all(own_proj, 'view', split_axis=0, concat_axis=0, tiled=True)  10.2 us
    reduce_sum x16, other arithmetic, composite(): totals = jnp.sum(log_keep, axis=2)  9.52 us
  transfers between devices with their start and end apart: 5, of which 5 were waited for; matrix products, arithmetic and copies ran while one was open for 3% of the time, Pallas kernels for 0%

commit v1 on v0

v1 whole, which is shorter than its diff:
```python
import jax
import jax.numpy as jnp
from jax import lax
from jax.experimental import pallas as pl
from jax.experimental.pallas import tpu as pltpu
from jax.sharding import PartitionSpec as P

PIX = 256
TILE_COLS = 32
G = 128
FEAT = 9
F32 = jnp.float32
BF16 = jnp.bfloat16
LOG2E = 1.4426950408889634

SH_ZERO = 0.28209479177387814
SH_ONE = 0.4886025119029199
SH_TWO = (
    1.0925484305920792,
    -1.0925484305920792,
    0.31539156525252005,
    -1.0925484305920792,
    0.5462742152960396,
)
SH_THREE = (
    -0.5900435899266435,
    2.890611442640554,
    -0.4570457994644658,
    0.3731763325901154,
    -0.4570457994644658,
    1.445305721320277,
    -0.5900435899266435,
)


def harmonics(dir_x, dir_y, dir_z):
    sq_x, sq_y, sq_z = (dir_x * dir_x, dir_y * dir_y, dir_z * dir_z)
    return [
        SH_ZERO * jnp.ones_like(dir_x),
        -SH_ONE * dir_y,
        SH_ONE * dir_z,
        -SH_ONE * dir_x,
        SH_TWO[0] * dir_x * dir_y,
        SH_TWO[1] * dir_y * dir_z,
        SH_TWO[2] * (2.0 * sq_z - sq_x - sq_y),
        SH_TWO[3] * dir_x * dir_z,
        SH_TWO[4] * (sq_x - sq_y),
        SH_THREE[0] * dir_y * (3.0 * sq_x - sq_y),
        SH_THREE[1] * dir_x * dir_y * dir_z,
        SH_THREE[2] * dir_y * (4.0 * sq_z - sq_x - sq_y),
        SH_THREE[3] * dir_z * (2.0 * sq_z - 3.0 * sq_x - 3.0 * sq_y),
        SH_THREE[4] * dir_x * (4.0 * sq_z - sq_x - sq_y),
        SH_THREE[5] * dir_z * (sq_x - sq_y),
        SH_THREE[6] * dir_x * (sq_x - 3.0 * sq_y),
    ]


def project(position, log_scales, quats, logit, coefs, cam):
    rotation = [[cam[3 * row + col] for col in range(3)] for row in range(3)]
    translation = cam[9:12]
    focal_x, focal_y, centre_x, centre_y = cam[12:16]
    view_pos = [
        rotation[row][0] * position[0]
        + rotation[row][1] * position[1]
        + rotation[row][2] * position[2]
        + translation[row]
        for row in range(3)
    ]
    inv_depth = 1.0 / view_pos[2]
    quat_w = quats[0] + 3.0
    quat_x, quat_y, quat_z = quats[1:4]
    quat_norm = jnp.sqrt(quat_w * quat_w + quat_x * quat_x + quat_y * quat_y + quat_z * quat_z)
    inv_norm = 1.0 / quat_norm
    quat_w, quat_x, quat_y, quat_z = (
        quat_w * inv_norm,
        quat_x * inv_norm,
        quat_y * inv_norm,
        quat_z * inv_norm,
    )
    spin = [
        [
            1.0 - 2.0 * (quat_y * quat_y + quat_z * quat_z),
            2.0 * (quat_x * quat_y - quat_w * quat_z),
            2.0 * (quat_x * quat_z + quat_w * quat_y),
        ],
        [
            2.0 * (quat_x * quat_y + quat_w * quat_z),
            1.0 - 2.0 * (quat_x * quat_x + quat_z * quat_z),
            2.0 * (quat_y * quat_z - quat_w * quat_x),
        ],
        [
            2.0 * (quat_x * quat_z - quat_w * quat_y),
            2.0 * (quat_y * quat_z + quat_w * quat_x),
            1.0 - 2.0 * (quat_x * quat_x + quat_y * quat_y),
        ],
    ]
    scales = [jnp.exp(row) for row in log_scales]
    world = [[spin[row][col] * scales[col] for col in range(3)] for row in range(3)]
    step_x = focal_x * inv_depth
    step_y = focal_y * inv_depth
    slide_x = step_x * view_pos[0] * inv_depth
    slide_y = step_y * view_pos[1] * inv_depth
    jac = [
        [step_x * rotation[0][col] - slide_x * rotation[2][col] for col in range(3)],
        [step_y * rotation[1][col] - slide_y * rotation[2][col] for col in range(3)],
    ]
    screen = [
        [
            jac[row][0] * world[0][col] + jac[row][1] * world[1][col] + jac[row][2] * world[2][col]
            for col in range(3)
        ]
        for row in range(2)
    ]
    sigma_xx = screen[0][0] * screen[0][0] + screen[0][1] * screen[0][1] + screen[0][2] * screen[0][2] + 0.3
    sigma_yy = screen[1][0] * screen[1][0] + screen[1][1] * screen[1][1] + screen[1][2] * screen[1][2] + 0.3
    sigma_xy = screen[0][0] * screen[1][0] + screen[0][1] * screen[1][1] + screen[0][2] * screen[1][2]
    inv_det = 1.0 / (sigma_xx * sigma_yy - sigma_xy * sigma_xy)
    screen_x = step_x * view_pos[0] + centre_x
    screen_y = step_y * view_pos[1] + centre_y
    opacity = 1.0 / (1.0 + jnp.exp(-logit))
    eye = [
        -(
            rotation[0][col] * translation[0]
            + rotation[1][col] * translation[1]
            + rotation[2][col] * translation[2]
        )
        for col in range(3)
    ]
    offs = [position[col] - eye[col] for col in range(3)]
    inv_dist = 1.0 / jnp.sqrt(offs[0] * offs[0] + offs[1] * offs[1] + offs[2] * offs[2])
    basis = harmonics(offs[0] * inv_dist, offs[1] * inv_dist, offs[2] * inv_dist)
    colours = []
    for channel in range(3):
        total = basis[0] * coefs[channel]
        for band in range(1, 16):
            total = total + basis[band] * coefs[3 * band + channel]
        colours.append(jnp.maximum(0.5 + total, 0.0))
    return [
        screen_x,
        screen_y,
        sigma_yy * inv_det,
        -sigma_xy * inv_det,
        sigma_xx * inv_det,
        opacity,
    ] + colours


def block_inputs(refs, block, views):
    means, log_scales, rotations, logits, coefs = refs

    def rows(ref, count):
        return [jnp.broadcast_to(ref[block, pl.ds(r, 1), :], (views, G)) for r in range(count)]

    return (rows(means, 3), rows(log_scales, 3), rows(rotations, 4), rows(logits, 1)[0], rows(coefs, 48))


def camera_columns(cam_ref, views):
    cams = cam_ref[...]
    return [jnp.broadcast_to(cams[:, col : col + 1], (views, G)) for col in range(16)]


def project_kernel(means, log_scales, rotations, logits, coefs, cam_ref, out_ref):
    views = cam_ref.shape[0]
    blocks = means.shape[0]
    cam = camera_columns(cam_ref, views)
    for block in range(blocks):
        pieces = block_inputs((means, log_scales, rotations, logits, coefs), block, views)
        for feat, value in enumerate(project(*pieces, cam)):
            out_ref[pl.ds(block * FEAT + feat, views, stride=blocks * FEAT), :] = value


def unproject_kernel(
    means, log_scales, rotations, logits, coefs, cam_ref, back_ref, o_means, o_scales, o_rot, o_logit, o_coef
):
    views = cam_ref.shape[0]
    blocks = means.shape[0]
    cam = camera_columns(cam_ref, views)

    def total(value):
        return jnp.sum(value, axis=0, keepdims=True)

    for block in range(blocks):
        pieces = block_inputs((means, log_scales, rotations, logits, coefs), block, views)
        _, pull = jax.vjp(lambda *own: project(*own, cam), *pieces)
        seeds = [
            back_ref[pl.ds(block * FEAT + feat, views, stride=blocks * FEAT), :] for feat in range(FEAT)
        ]
        g_means, g_scales, g_rot, g_logit, g_coef = pull(seeds)
        for ref, rows in ((o_means, g_means), (o_scales, g_scales), (o_rot, g_rot), (o_logit, [g_logit]), (o_coef, g_coef)):
            for row, value in enumerate(rows):
                ref[block, pl.ds(row, 1), :] = total(value)


def gather_kernel(picks, src_ref, out_ref):
    renderers, cap = picks.shape
    for r in range(renderers):
        for c in range(cap):
            pick = jnp.maximum(picks[r, c], 0)
            out_ref[pl.ds((r * cap + c) * FEAT, FEAT), :] = src_ref[pl.ds(pick * FEAT, FEAT), :]


def scatter_kernel(picks, src_ref, out_ref, expo_ref):
    renderers, cap = picks.shape
    stride = cap * FEAT + 1
    out_ref[...] = jnp.zeros(out_ref.shape, F32)
    for r in range(renderers):
        for c in range(cap):
            pick = jnp.maximum(picks[r, c], 0)
            place = pl.ds(pick * FEAT, FEAT)
            out_ref[place, :] = out_ref[place, :] + src_ref[pl.ds(r * stride + c * FEAT, FEAT), :]
    terms = src_ref[pl.ds(stride - 1, renderers, stride=stride), :]
    expo_ref[...] = jnp.sum(terms, axis=0, keepdims=True)[:, 0:12]


def split2(value):
    high = value.astype(BF16)
    low = (value - high.astype(F32)).astype(BF16)
    return high, low


def monomials(part, pixel):
    spot_x = (pixel % 16).astype(F32) - 7.5
    spot_y = (pixel // 16).astype(F32) - 7.5
    value = jnp.where(part == 0, 1.0, 0.0)
    value = jnp.where(part == 1, spot_x, value)
    value = jnp.where(part == 2, spot_y, value)
    value = jnp.where(part == 3, spot_x * spot_x, value)
    value = jnp.where(part == 4, spot_x * spot_y, value)
    return jnp.where(part == 5, spot_y * spot_y, value)


def dot(left, right):
    return jnp.dot(left, right, preferred_element_type=F32)


def render_kernel(
    tile_ids,
    slots,
    expo,
    in_ref,
    goal_ref,
    shown_ref,
    grad_ref,
    raw,
    mat,
    mat_h,
    mat_m,
    left,
    mono,
    mono_t,
    al0,
    al1,
    wt0,
    wt1,
    gm0,
    gm1,
    wt_h,
    wt_l,
    ccol,
    gall,
    gsplit,
    gtr,
):
    tiles, kmax = slots.shape
    groups = tiles // 8
    picks = tiles * kmax
    cap = 2
    stride = cap * FEAT + 1
    scene = grad_ref.shape[0] // stride
    rows16 = lax.broadcasted_iota(jnp.int32, (16, G), 0)
    lanes = lax.broadcasted_iota(jnp.int32, (1, G), 1)
    alphas, weights, slopes = (al0, al1), (wt0, wt1), (gm0, gm1)

    part = lax.broadcasted_iota(jnp.int32, (G, PIX), 0) % 16
    pixel = lax.broadcasted_iota(jnp.int32, (G, PIX), 1)
    table = monomials(part, pixel).astype(BF16)
    for piece in range(3):
        mono[piece * G : (piece + 1) * G, :] = table
    part_t = lax.broadcasted_iota(jnp.int32, (PIX, G), 1) % 16
    pixel_t = lax.broadcasted_iota(jnp.int32, (PIX, G), 0)
    table_t = monomials(part_t, pixel_t).astype(BF16)
    mono_t[0:PIX, :] = table_t
    mono_t[PIX : 2 * PIX, :] = table_t

    def place(group, k, t):
        return (group * kmax + k) * 8 + t

    for group in range(groups):
        for t in range(8):
            tile = group * 8 + t
            tile_id = tile_ids[tile]
            mid_x = ((tile_id % TILE_COLS) * 16 + 8).astype(F32)
            mid_y = ((tile_id // TILE_COLS) * 16 + 8).astype(F32)
            shift = jnp.where(rows16 == 0, mid_x, jnp.where(rows16 == 1, mid_y, 0.0))
            for k in range(kmax):
                slot = slots[tile, k]
                base = jnp.maximum(slot, 0) * FEAT
                spot = place(group, k, t) * 16
                raw[spot : spot + FEAT, :] = in_ref[pl.ds(base, FEAT), :] - shift[0:FEAT]
                raw[spot + FEAT : spot + FEAT + 1, :] = jnp.full((1, G), jnp.where(slot < 0, -4000.0, 0.0))

    def feature(index):
        return raw[pl.ds(index, picks, stride=16), :]

    off_x, off_y, con_a, con_b, con_c, opac = [feature(i) for i in range(6)]
    poly_a = con_a * (-0.5 * LOG2E)
    poly_b = con_b * (-LOG2E)
    poly_c = con_c * (-0.5 * LOG2E)
    lead = poly_a * off_x + poly_b * off_y
    tail = poly_c * off_y
    coefs = [
        off_x * lead + off_y * tail + jnp.log(opac) * LOG2E + feature(FEAT),
        -(lead + poly_a * off_x),
        -(2.0 * tail + poly_b * off_x),
        poly_a,
        poly_b,
        poly_c,
    ]
    mat[...] = jnp.zeros(mat.shape, F32)
    for index in range(6):
        mat[pl.ds(index, picks, stride=16), :] = coefs[index]
    for channel in range(3):
        mat[pl.ds(8 + channel, picks, stride=16), :] = feature(6 + channel)
    whole = mat[...]
    high, low = split2(whole)
    mat_h[...] = high
    mat_m[...] = low

    for group in range(groups):
        for k in range(kmax):
            chunk = group * kmax + k
            turned = mat[chunk * G : (chunk + 1) * G, :].T
            first = turned.astype(BF16)
            rest = turned - first.astype(F32)
            second = rest.astype(BF16)
            third = (rest - second.astype(F32)).astype(BF16)
            trio = jnp.concatenate([first, second, third], axis=1)
            left[chunk * G : (chunk + 1) * G, :] = trio
            lanes3 = lax.broadcasted_iota(jnp.int32, (1, 3 * G), 1) % G
            for t in range(8):
                mask = jnp.where(lanes3 // 16 == t, 1.0, 0.0).astype(BF16)
                alpha = jnp.exp2(dot(trio * mask, mono[...]))
                for half in range(2):
                    alphas[half][pl.ds(chunk * G * 8 + t, G, stride=8), :] = alpha[:, half * G : (half + 1) * G]

    count = kmax * G

    def forward(step, keeps):
        keeps = list(keeps)
        for group in range(groups):
            row = pl.multiple_of((group * count + step) * 8, 8)
            for half in range(2):
                at = group * 2 + half
                weight = keeps[at] * alphas[half][pl.ds(row, 8), :]
                weights[half][pl.ds(row, 8), :] = weight
                keeps[at] = keeps[at] - weight
        return tuple(keeps)

    ones = jnp.ones((8, G), F32)
    lax.fori_loop(0, count, forward, (ones,) * (2 * groups), unroll=8)

    for group in range(groups):
        for t in range(8):
            total = jnp.zeros((16, PIX), F32)
            for k in range(kmax):
                spot = place(group, k, t)
                rows = pl.ds((group * kmax + k) * G * 8 + t, G, stride=8)
                weight = jnp.concatenate([weights[0][rows, :], weights[1][rows, :]], axis=1)
                w_high, w_low = split2(weight)
                wt_h[spot * G : (spot + 1) * G, :] = w_high
                wt_l[spot * G : (spot + 1) * G, :] = w_low
                m_high = mat_h[spot * 16 : spot * 16 + 16, :]
                m_low = mat_m[spot * 16 : spot * 16 + 16, :]
                both = dot(jnp.concatenate([m_high, m_low], axis=0), w_high)
                total = total + both[0:16] + both[16:32] + dot(m_high, w_low)
            for channel in range(3):
                row = channel * tiles + group * 8 + t
                ccol[row : row + 1, :] = total[8 + channel : 9 + channel, :]

    colour = [ccol[c * tiles : (c + 1) * tiles, :] for c in range(3)]
    miss = []
    for i in range(3):
        value = colour[i] + expo[0, 9 + i]
        for j in range(3):
            value = value + expo[0, 3 * i + j] * colour[j]
        shown_ref[:, i, :] = value
        miss.append(value - goal_ref[:, i, :])
    slope = []
    for j in range(3):
        value = miss[j]
        for i in range(3):
            value = value + expo[0, 3 * i + j] * miss[i]
        slope.append(value)
    terms = [miss[i] * colour[j] for i in range(3) for j in range(3)] + miss
    expo_row = jnp.zeros((1, G), F32)
    for index, value in enumerate(terms):
        folded = jnp.sum(value[:, 0:G] + value[:, G : 2 * G], axis=0, keepdims=True)
        expo_row = jnp.where(lanes == index, jnp.sum(folded, axis=1, keepdims=True), expo_row)

    for group in range(groups):
        base = group * 3 * G
        for half in range(2):
            side = slice(half * G, (half + 1) * G)
            highs, lows = [], []
            for channel in range(3):
                value = slope[channel][group * 8 : group * 8 + 8, side]
                s_high = value.astype(BF16).astype(F32)
                highs.append(s_high)
                lows.append(value - s_high)
            gall[...] = jnp.zeros(gall.shape, F32)
            for channel in range(3):
                gall[pl.ds(8 + channel, 8, stride=16), :] = lows[channel]
            gsplit[base + 2 * G : base + 3 * G, side] = gall[...].astype(BF16)
            for channel in range(3):
                gall[pl.ds(8 + channel, 8, stride=16), :] = highs[channel]
            g_high = gall[...].astype(BF16)
            gsplit[base : base + G, side] = g_high
            gsplit[base + G : base + 2 * G, side] = g_high
            for channel in range(3):
                gall[pl.ds(11 + channel, 8, stride=16), :] = lows[channel]
            turned = gall[...].T.astype(BF16)
            start = group * 2 * PIX + half * G
            gtr[start : start + G, :] = turned
            gtr[start + PIX : start + PIX + G, :] = turned
        g_rhs = gsplit[base : base + 3 * G, :]
        for k in range(kmax):
            chunk = group * kmax + k
            first = left[chunk * G : (chunk + 1) * G, 0:G]
            second = left[chunk * G : (chunk + 1) * G, G : 2 * G]
            trio = jnp.concatenate([first, second, first], axis=1)
            lanes3 = lax.broadcasted_iota(jnp.int32, (1, 3 * G), 1) % G
            for t in range(8):
                mask = jnp.where(lanes3 // 16 == t, 1.0, 0.0).astype(BF16)
                value = dot(trio * mask, g_rhs)
                for half in range(2):
                    slopes[half][pl.ds(chunk * G * 8 + t, G, stride=8), :] = value[:, half * G : (half + 1) * G]

    def backward(step, behind):
        behind = list(behind)
        for group in range(groups):
            row = pl.multiple_of((group * count + (count - 1 - step)) * 8, 8)
            for half in range(2):
                at = group * 2 + half
                gap = slopes[half][pl.ds(row, 8), :] - behind[at]
                slopes[half][pl.ds(row, 8), :] = weights[half][pl.ds(row, 8), :] * gap
                behind[at] = behind[at] + alphas[half][pl.ds(row, 8), :] * gap
        return tuple(behind)

    zeros = jnp.zeros((8, G), F32)
    lax.fori_loop(0, count, backward, (zeros,) * (2 * groups), unroll=8)

    lane_tile = lax.broadcasted_iota(jnp.int32, (G, G), 1) // 16
    for group in range(groups):
        g_t = gtr[group * 2 * PIX : (group + 1) * 2 * PIX, :]
        for k in range(kmax):
            chunk = group * kmax + k
            acc = jnp.zeros((G, G), F32)
            for t in range(8):
                spot = place(group, k, t)
                rows = pl.ds(chunk * G * 8 + t, G, stride=8)
                value = jnp.concatenate([slopes[0][rows, :], slopes[1][rows, :]], axis=1)
                v_high, v_low = split2(value)
                out = dot(jnp.concatenate([v_high, v_low], axis=1), mono_t[...])
                w_high = wt_h[spot * G : (spot + 1) * G, :]
                w_low = wt_l[spot * G : (spot + 1) * G, :]
                out = out + dot(jnp.concatenate([w_high, w_low], axis=1), g_t)
                acc = jnp.where(lane_tile == t, out, acc)
            mat[chunk * G : (chunk + 1) * G, :] = acc.T

    def moment(index):
        return mat[pl.ds(index, picks, stride=16), :]

    sum_0, sum_x, sum_y, sum_xx, sum_xy, sum_yy = [moment(i) for i in range(6)]
    off_x, off_y, con_a, con_b, con_c, opac = [feature(i) for i in range(6)]
    cen_x = sum_x - off_x * sum_0
    cen_y = sum_y - off_y * sum_0
    cen_xx = sum_xx - off_x * (sum_x + cen_x)
    cen_yy = sum_yy - off_y * (sum_y + cen_y)
    cen_xy = sum_xy - off_x * sum_y - off_y * cen_x
    outs = [
        con_a * cen_x + con_b * cen_y,
        con_b * cen_x + con_c * cen_y,
        -0.5 * cen_xx,
        -cen_xy,
        -0.5 * cen_yy,
        sum_0 / opac,
    ] + [moment(8 + c) + moment(11 + c) for c in range(3)]
    for index, value in enumerate(outs):
        raw[pl.ds(index, picks, stride=16), :] = value

    grad_ref[...] = jnp.zeros(grad_ref.shape, F32)
    for group in range(groups):
        for k in range(kmax):
            for t in range(8):
                slot = jnp.maximum(slots[group * 8 + t, k], 0)
                where = pl.ds((slot // cap) * stride + (slot % cap) * FEAT, FEAT)
                spot = place(group, k, t) * 16
                grad_ref[where, :] = grad_ref[where, :] + raw[spot : spot + FEAT, :]
    grad_ref[pl.ds(stride - 1, scene, stride=stride), :] = jnp.broadcast_to(expo_row, (scene, G))


def vmem():
    return pl.BlockSpec(memory_space=pltpu.VMEM)


def smem():
    return pl.BlockSpec(memory_space=pltpu.SMEM)


def across(rows, axis, parts):
    shaped = rows.reshape(parts, rows.shape[0] // parts, 1, G)
    moved = lax.all_to_all(shaped, axis, split_axis=0, concat_axis=0, tiled=True)
    return moved.reshape(rows.shape)


def render(tile_ids, slots, expo, incoming, goal, interpret=False):
    tiles, kmax = slots.shape
    picks = tiles * kmax
    groups = tiles // 8
    scene = incoming.shape[0] // (2 * FEAT)
    big = pltpu.VMEM((picks * G, G), F32)
    return pl.pallas_call(
        render_kernel,
        out_shape=(
            jax.ShapeDtypeStruct((tiles, 3, PIX), F32),
            jax.ShapeDtypeStruct((scene * (2 * FEAT + 1), G), F32),
        ),
        in_specs=[smem(), smem(), smem(), vmem(), vmem()],
        out_specs=(vmem(), vmem()),
        scratch_shapes=[
            pltpu.VMEM((picks * 16, G), F32),
            pltpu.VMEM((picks * 16, G), F32),
            pltpu.VMEM((picks * 16, G), BF16),
            pltpu.VMEM((picks * 16, G), BF16),
            pltpu.VMEM((groups * kmax * G, 3 * G), BF16),
            pltpu.VMEM((3 * G, PIX), BF16),
            pltpu.VMEM((2 * PIX, G), BF16),
            big,
            big,
            big,
            big,
            big,
            big,
            pltpu.VMEM((picks * G, PIX), BF16),
            pltpu.VMEM((picks * G, PIX), BF16),
            pltpu.VMEM((3 * tiles, PIX), F32),
            pltpu.VMEM((G, G), F32),
            pltpu.VMEM((groups * 3 * G, PIX), BF16),
            pltpu.VMEM((groups * 2 * PIX, G), BF16),
        ],
        compiler_params=pltpu.CompilerParams(vmem_limit_bytes=56 * 1024 * 1024),
        name="render",
        interpret=interpret,
    )(tile_ids, slots, expo, incoming, goal)


def local(
    means,
    log_scales,
    rotations,
    opacity_logits,
    colour_coefs,
    cameras,
    exposure,
    target,
    tile_ids,
    send_list,
    pair_slots,
):
    views = lax.axis_size("view")
    scene = lax.axis_size("scene")
    blocks = means.shape[0]
    cap = send_list.shape[3]
    pieces = (means, log_scales, rotations, opacity_logits, colour_coefs)
    picks = send_list[0, 0]
    own_rows = jax.ShapeDtypeStruct((views * blocks * FEAT, G), F32)
    own_proj = pl.pallas_call(
        project_kernel,
        out_shape=own_rows,
        in_specs=[vmem()] * 6,
        out_specs=vmem(),
        name="project",
    )(*pieces, cameras)
    projected = across(own_proj, "view", views)
    outgoing = pl.pallas_call(
        gather_kernel,
        out_shape=jax.ShapeDtypeStruct((scene * cap * FEAT, G), F32),
        in_specs=[smem(), vmem()],
        out_specs=vmem(),
        name="gather",
    )(picks, projected)
    incoming = across(outgoing, "scene", scene)
    shown, grad_rows = render(tile_ids[0], pair_slots[0], exposure, incoming, target[0])
    returned = across(grad_rows, "scene", scene)
    grad_proj, grad_expo = pl.pallas_call(
        scatter_kernel,
        out_shape=(own_rows, jax.ShapeDtypeStruct((1, 12), F32)),
        in_specs=[smem(), vmem()],
        out_specs=(vmem(), vmem()),
        name="scatter",
    )(picks, returned)
    sent_back = across(grad_proj, "view", views)
    grads = pl.pallas_call(
        unproject_kernel,
        out_shape=tuple(jax.ShapeDtypeStruct(piece.shape, F32) for piece in pieces),
        in_specs=[vmem()] * 7,
        out_specs=tuple(vmem() for _ in pieces),
        name="unproject",
    )(*pieces, cameras, sent_back)
    return (shown[None], *grads, grad_expo)


def solution(mesh):
    return jax.shard_map(
        local,
        mesh=mesh,
        in_specs=(
            P(("view", "scene"), None, None),
            P(("view", "scene"), None, None),
            P(("view", "scene"), None, None),
            P(("view", "scene"), None, None),
            P(("view", "scene"), None, None),
            P(),
            P("view", None),
            P("view", "scene", None, None),
            P("view", "scene"),
            P("view", "scene", None, None),
            P("view", "scene", None),
        ),
        out_specs=(
            P("view", "scene", None, None),
            P(("view", "scene"), None, None),
            P(("view", "scene"), None, None),
            P(("view", "scene"), None, None),
            P(("view", "scene"), None, None),
            P(("view", "scene"), None, None),
            P("view", None),
        ),
        check_vma=False,
    )
```

time: 327 us -> 153 us (0.47)
  matrix products: 91 us -> 0 us
  loops' own time: 43.7 us -> 0 us
  blocking collectives: 0 us -> 42.2 us
  waiting for transfers between devices: 77.2 us -> 38.3 us
  Pallas kernels: 0 us -> 30.5 us
  other arithmetic: 30.2 us -> 0 us
  local copies, waits for them, and re-layouts: 34.3 us -> 9.16 us
  starting transfers between devices: 48 us -> 31.4 us
    dot_general x128 -> x0, matrix products: 91 us -> none  [the longest x32 41.3 us: composite(): jnp.dot(log_keep.reshape(-1, lane_count), strict, precision=lax.Precision...]
    another operation x1 -> x0, loops' own time: 43.7 us -> none  [local(): lax.map(render_tile, (tile_ids[0], pair_slots[0], target[0]))]
    all_to_all x0 -> x1, blocking collectives: none -> 42.2 us  [across(): lax.all_to_all(shaped, axis, split_axis=0, concat_axis=0, tiled=True)]
    all_to_all x5 -> x3, waiting for transfers between devices: 77.2 us -> 38.3 us  [across(): lax.all_to_all(shaped, axis, split_axis=0, concat_axis=0, tiled=True)]
    pallas_call x0 -> x5, Pallas kernels: none -> 30.5 us  [the longest x1 22.1 us: render(): pl.pallas_call(render_kernel, out_shape=(jax.ShapeDtypeStruct((tiles, 3,...]
    all_to_all x5 -> x3, starting transfers between devices: 48 us -> 31.4 us  [across(): lax.all_to_all(shaped, axis, split_axis=0, concat_axis=0, tiled=True)]
    reduce_sum x24 -> x0, other arithmetic: 10.7 us -> none  [the longest x16 9.52 us: composite(): totals = jnp.sum(log_keep, axis=2)]
    gather x17 -> x0, local copies, waits for them, and re-layouts: 9.57 us -> none  [the longest x16 8.81 us: render_tile(): chosen = jnp.take(incoming, jnp.maximum(slot_list, 0), axis=0)]
  transfers between devices with their start and end apart: 5 -> 3, of which waited for: 5 -> 3; matrix products, arithmetic and copies ran while one was open for 3% -> 2% of each run, Pallas kernels for 0% -> 0%
where the time goes in v1:
time: 153 us; the launch traced here: 152 us
  blocking collectives  42.2 us (28%)
  waiting for transfers between devices  38.3 us (25%)
  starting transfers between devices  31.4 us (21%)
  Pallas kernels  30.5 us (20%)
  local copies, waits for them, and re-layouts  9.16 us (6%)
    all_to_all x1, blocking collectives, across(): lax.all_to_all(shaped, axis, split_axis=0, concat_axis=0, tiled=True)  42.2 us
    all_to_all x3, waiting for transfers between devices, across(): lax.all_to_all(shaped, axis, split_axis=0, concat_axis=0, tiled=True)  38.3 us
    all_to_all x3, starting transfers between devices, across(): lax.all_to_all(shaped, axis, split_axis=0, concat_axis=0, tiled=True)  31.4 us
    pallas_call x1, Pallas kernels, render(): pl.pallas_call(render_kernel, out_shape=(jax.ShapeDtypeStruct((tiles, 3,...  22.1 us
    unnamed x24, local copies, waits for them, and re-layouts  7.77 us
  transfers between devices with their start and end apart: 3, of which 3 were waited for; matrix products, arithmetic and copies ran while one was open for 2% of the time, Pallas kernels for 0%

profile of v1, /device:TPU:1, one launch (start us, length us, event | category | flops | bytes accessed | tf_op | source)
XLA Modules:
  0.0 152.2 jit_solution(10356063067112792296)
XLA Ops:
  0.6 1.3 copy.40.means
  1.9 0.6 copy.41.log_scales
  2.5 1.6 %project.1 = f32[144,128]{1,0:T(8,128)} custom-call(f32[2,3,128]{2,1,0:T(4,128)} %copy.40.means, f32[2,3,128]{2,1,0:T(4,128)} %copy.41.log_scales, f32[2,4,128]{2,1,0:T(4,128)} %rotations.3, f32[2,1,128]{2,1,0:T(1,128)} %logits.3, f32[2,48,128]{2,1,0:T(8,128)} %coefs.3, f32[8,16]{1,0:T(8,128)} %cam_ref.3), custom_call_target="tpu_custom_call" | custom-call | tf_op jit(solution)/shard_map/project/pallas_call | solution.py:577
  4.2 10.1 %all-to-all-start = ((f32[8,18,1,128]{3,2,1,0:T(1,128)}), f32[8,18,1,128]{3,2,1,0:T(1,128)S(1)}, u32[]{:S(2)}, u32[]{:S(2)}) async-start(f32[8,18,1,128]{3,2,1,0:T(1,128)} %bitcast.20), calls=%async_computation | async-start | bytes 147456 | tf_op jit(solution)/shard_map/all_to_all | solution.py:512
  14.3 0.7 copy-done.8
  14.9 0.7 copy.43.picks
  15.6 3.5 %all-to-all-done = f32[8,18,1,128]{3,2,1,0:T(1,128)S(1)} async-done(((f32[8,18,1,128]{3,2,1,0:T(1,128)}), f32[8,18,1,128]{3,2,1,0:T(1,128)S(1)}, u32[]{:S(2)}, u32[]{:S(2)}) %all-to-all-start) | async-done | bytes 73760 | tf_op jit(solution)/shard_map/all_to_all | solution.py:512
  19.2 0.6 copy-done.2
  19.8 2.2 %gather.1 = f32[1152,128]{1,0:T(8,128)} custom-call(s32[64,2]{1,0:T(8,128)} %copy.43.picks, f32[144,128]{1,0:T(8,128)} %bitcast.21), custom_call_target="tpu_custom_call" | custom-call | tf_op jit(solution)/shard_map/gather/pallas_call | solution.py:585
  22.0 14.3 %all-to-all-start.1 = ((f32[64,18,1,128]{3,2,1,0:T(1,128)}), f32[64,18,1,128]{3,2,1,0:T(1,128)S(1)}, u32[]{:S(2)}, u32[]{:S(2)}) async-start(f32[64,18,1,128]{3,2,1,0:T(1,128)} %bitcast.17), calls=%async_computation.1 | async-start | bytes 1179648 | tf_op jit(solution)/shard_map/all_to_all | solution.py:512
  36.3 0.7 copy.46.slots
  37.0 0.6 copy.56
  37.6 30.6 %all-to-all-done.1 = f32[64,18,1,128]{3,2,1,0:T(1,128)S(1)} async-done(((f32[64,18,1,128]{3,2,1,0:T(1,128)}), f32[64,18,1,128]{3,2,1,0:T(1,128)S(1)}, u32[]{:S(2)}, u32[]{:S(2)}) %all-to-all-start.1) | async-done | bytes 589856 | tf_op jit(solution)/shard_map/all_to_all | solution.py:512
  68.2 0.8 copy-done
  69.0 22.1 %render.1 = (f32[16,3,256]{2,1,0:T(4,128)}, f32[1216,128]{1,0:T(8,128)}) custom-call(s32[16]{0:T(128)} %bitcast.27, s32[16,4]{1,0:T(8,128)} %copy.46.slots, f32[1,12]{1,0:T(1,128)} %expo.1, f32[1152,128]{1,0:T(8,128)} %bitcast.16, f32[16,3,256]{2,1,0:T(4,128)} %bitcast.22), custom_call_target="tpu_custom_call" | custom-call | tf_op jit(solution)/shard_map/render/pallas_call | solution.py:522
  91.1 42.2 %all_to_all.20 = f32[64,19,1,128]{3,2,1,0:T(1,128)} all-to-all(f32[64,19,1,128]{3,2,1,0:T(1,128)} %bitcast.18), channel_id=1, replica_groups=mesh['view'=8,'scene'=64] {'scene'}, dimensions={0} | all-to-all | bytes 1245184 | tf_op jit(solution)/shard_map/all_to_all | solution.py:512
  133.3 2.5 %scatter.1 = (f32[144,128]{1,0:T(8,128)}, f32[1,12]{1,0:T(1,128)}) custom-call(s32[64,2]{1,0:T(8,128)} %copy.43.picks, f32[1216,128]{1,0:T(8,128)} %bitcast.15), custom_call_target="tpu_custom_call" | custom-call | tf_op jit(solution)/shard_map/scatter/pallas_call | solution.py:595
  135.8 7.1 %all-to-all-start.3 = ((f32[8,18,1,128]{3,2,1,0:T(1,128)}), f32[8,18,1,128]{3,2,1,0:T(1,128)S(1)}, u32[]{:S(2)}, u32[]{:S(2)}) async-start(f32[8,18,1,128]{3,2,1,0:T(1,128)} %bitcast.23), calls=%async_computation.3 | async-start | bytes 147456 | tf_op jit(solution)/shard_map/all_to_all | solution.py:512
  142.8 0.6 copy.52
  143.5 4.3 %all-to-all-done.3 = f32[8,18,1,128]{3,2,1,0:T(1,128)S(1)} async-done(((f32[8,18,1,128]{3,2,1,0:T(1,128)}), f32[8,18,1,128]{3,2,1,0:T(1,128)S(1)}, u32[]{:S(2)}, u32[]{:S(2)}) %all-to-all-start.3) | async-done | bytes 73760 | tf_op jit(solution)/shard_map/all_to_all | solution.py:512
  147.7 0.6 copy-done.1
  148.4 2.0 %unproject.1 = (f32[2,3,128]{2,1,0:T(4,128)}, f32[2,3,128]{2,1,0:T(4,128)}, f32[2,4,128]{2,1,0:T(4,128)}, f32[2,1,128]{2,1,0:T(1,128)}, f32[2,48,128]{2,1,0:T(8,128)}) custom-call(f32[2,3,128]{2,1,0:T(4,128)} %copy.40.means, f32[2,3,128]{2,1,0:T(4,128)} %copy.41.log_scales, f32[2,4,128]{2,1,0:T(4,128)} %rotations.3, f32[2,1,128]{2,1,0:T(1,128)} %logits.3, ...), custom_call_target="tpu_custom_call" | custom-call | tf_op jit(solution)/shard_map/unproject/pallas_call | solution.py:603
  150.4 1.3 copy.53
  151.7 0.6 copy.54
  (14 shorter events, 0.0 us)
Async XLA Ops:
  0.6 1.3 copy-start.6
  4.2 15.0 %all-to-all-start = ((f32[8,18,1,128]{3,2,1,0:T(1,128)}), f32[8,18,1,128]{3,2,1,0:T(1,128)S(1)}, u32[]{:S(2)}, u32[]{:S(2)}) async-start(f32[8,18,1,128]{3,2,1,0:T(1,128)} %bitcast.20), calls=%async_computation | async-start | bytes 147456 | tf_op jit(solution)/shard_map/all_to_all | solution.py:512
  14.3 0.7 copy-start.8
  19.2 0.6 copy-start.2
  22.0 14.3 %copy-start.7 = (s32[1,16,4]{1,2,0:T(4,128)S(1)}, s32[1,16,4]{1,2,0:T(4,128)}, u32[]{:S(2)}) copy-start(s32[1,16,4]{1,2,0:T(4,128)} %param.21) | copy-start | bytes 772
  22.0 15.0 %copy-start.4 = (f32[1,16,3,256]{3,1,2,0:T(8,128)S(1)}, f32[1,16,3,256]{3,1,2,0:T(8,128)}, u32[]{:S(2)}) copy-start(f32[1,16,3,256]{3,1,2,0:T(8,128)} %param.18) | copy-start | bytes 147460
  22.0 46.2 %all-to-all-start.1 = ((f32[64,18,1,128]{3,2,1,0:T(1,128)}), f32[64,18,1,128]{3,2,1,0:T(1,128)S(1)}, u32[]{:S(2)}, u32[]{:S(2)}) async-start(f32[64,18,1,128]{3,2,1,0:T(1,128)} %bitcast.17), calls=%async_computation.1 | async-start | bytes 1179648 | tf_op jit(solution)/shard_map/all_to_all | solution.py:512
  68.2 0.8 copy-start
  135.8 7.1 %copy-start.3 = (f32[16,3,256]{2,1,0:T(4,128)S(1)}, f32[16,3,256]{2,1,0:T(4,128)}, u32[]{:S(2)}) copy-start(f32[16,3,256]{2,1,0:T(4,128)} %get-tuple-element.16) | copy-start | bytes 147460
  135.8 12.0 %all-to-all-start.3 = ((f32[8,18,1,128]{3,2,1,0:T(1,128)}), f32[8,18,1,128]{3,2,1,0:T(1,128)S(1)}, u32[]{:S(2)}, u32[]{:S(2)}) async-start(f32[8,18,1,128]{3,2,1,0:T(1,128)} %bitcast.23), calls=%async_computation.3 | async-start | bytes 147456 | tf_op jit(solution)/shard_map/all_to_all | solution.py:512
  147.7 0.6 copy-start.1
  150.4 1.3 copy-start.5

commit v2 on v1

--- a/solution.py
+++ b/solution.py
@@ -151,7 +151,10 @@
     def rows(ref, count):
         return [jnp.broadcast_to(ref[block, pl.ds(r, 1), :], (views, G)) for r in range(count)]
 
-    return (rows(means, 3), rows(log_scales, 3), rows(rotations, 4), rows(logits, 1)[0], rows(coefs, 48))
+    def turned(ref):
+        return [jnp.broadcast_to(ref[r, pl.ds(block, 1), :], (views, G)) for r in range(3)]
+
+    return (turned(means), turned(log_scales), rows(rotations, 4), rows(logits, 1)[0], rows(coefs, 48))
 
 
 def camera_columns(cam_ref, views):
@@ -161,7 +164,7 @@
 
 def project_kernel(means, log_scales, rotations, logits, coefs, cam_ref, out_ref):
     views = cam_ref.shape[0]
-    blocks = means.shape[0]
+    blocks = rotations.shape[0]
     cam = camera_columns(cam_ref, views)
     for block in range(blocks):
         pieces = block_inputs((means, log_scales, rotations, logits, coefs), block, views)
@@ -173,7 +176,7 @@
     means, log_scales, rotations, logits, coefs, cam_ref, back_ref, o_means, o_scales, o_rot, o_logit, o_coef
 ):
     views = cam_ref.shape[0]
-    blocks = means.shape[0]
+    blocks = rotations.shape[0]
     cam = camera_columns(cam_ref, views)
 
     def total(value):
@@ -186,26 +189,29 @@
             back_ref[pl.ds(block * FEAT + feat, views, stride=blocks * FEAT), :] for feat in range(FEAT)
         ]
         g_means, g_scales, g_rot, g_logit, g_coef = pull(seeds)
-        for ref, rows in ((o_means, g_means), (o_scales, g_scales), (o_rot, g_rot), (o_logit, [g_logit]), (o_coef, g_coef)):
+        for ref, rows in ((o_means, g_means), (o_scales, g_scales)):
+            for row, value in enumerate(rows):
+                ref[row, pl.ds(block, 1), :] = total(value)
+        for ref, rows in ((o_rot, g_rot), (o_logit, [g_logit]), (o_coef, g_coef)):
             for row, value in enumerate(rows):
                 ref[block, pl.ds(row, 1), :] = total(value)
 
 
 def gather_kernel(picks, src_ref, out_ref):
-    renderers, cap = picks.shape
+    cap, renderers = picks.shape
     for r in range(renderers):
         for c in range(cap):
-            pick = jnp.maximum(picks[r, c], 0)
+            pick = jnp.maximum(picks[c, r], 0)
             out_ref[pl.ds((r * cap + c) * FEAT, FEAT), :] = src_ref[pl.ds(pick * FEAT, FEAT), :]
 
 
 def scatter_kernel(picks, src_ref, out_ref, expo_ref):
-    renderers, cap = picks.shape
+    cap, renderers = picks.shape
     stride = cap * FEAT + 1
     out_ref[...] = jnp.zeros(out_ref.shape, F32)
     for r in range(renderers):
         for c in range(cap):
-            pick = jnp.maximum(picks[r, c], 0)
+            pick = jnp.maximum(picks[c, r], 0)
             place = pl.ds(pick * FEAT, FEAT)
             out_ref[place, :] = out_ref[place, :] + src_ref[pl.ds(r * stride + c * FEAT, FEAT), :]
     terms = src_ref[pl.ds(stride - 1, renderers, stride=stride), :]
@@ -216,6 +222,13 @@
     high = value.astype(BF16)
     low = (value - high.astype(F32)).astype(BF16)
     return high, low
+
+
+def pieces3(value):
+    high = value.astype(BF16).astype(F32)
+    rest = value - high
+    middle = rest.astype(BF16).astype(F32)
+    return high, middle, rest - middle
 
 
 def monomials(part, pixel):
@@ -231,6 +244,13 @@
 
 def dot(left, right):
     return jnp.dot(left, right, preferred_element_type=F32)
+
+
+def dot_t(left, right):
+    return lax.dot_general(left, right, (((1,), (1,)), ((), ())), preferred_element_type=F32)
+
+
+ROWS = 32
 
 
 def render_kernel(
@@ -243,8 +263,8 @@
     grad_ref,
     raw,
     mat,
-    mat_h,
-    mat_m,
+    mat_c,
+    mat_b,
     left,
     mono,
     mono_t,
@@ -254,33 +274,32 @@
     wt1,
     gm0,
     gm1,
+    hh0,
+    hh1,
     wt_h,
     wt_l,
     ccol,
     gall,
-    gsplit,
-    gtr,
+    g_rhs,
+    g_own,
+    mom,
 ):
-    tiles, kmax = slots.shape
+    kmax, tiles = slots.shape
     groups = tiles // 8
     picks = tiles * kmax
     cap = 2
     stride = cap * FEAT + 1
     scene = grad_ref.shape[0] // stride
+    wide = 8 * ROWS
     rows16 = lax.broadcasted_iota(jnp.int32, (16, G), 0)
     lanes = lax.broadcasted_iota(jnp.int32, (1, G), 1)
-    alphas, weights, slopes = (al0, al1), (wt0, wt1), (gm0, gm1)
-
-    part = lax.broadcasted_iota(jnp.int32, (G, PIX), 0) % 16
-    pixel = lax.broadcasted_iota(jnp.int32, (G, PIX), 1)
-    table = monomials(part, pixel).astype(BF16)
-    for piece in range(3):
-        mono[piece * G : (piece + 1) * G, :] = table
-    part_t = lax.broadcasted_iota(jnp.int32, (PIX, G), 1) % 16
-    pixel_t = lax.broadcasted_iota(jnp.int32, (PIX, G), 0)
-    table_t = monomials(part_t, pixel_t).astype(BF16)
-    mono_t[0:PIX, :] = table_t
-    mono_t[PIX : 2 * PIX, :] = table_t
+    alphas, weights, slopes, moved = (al0, al1), (wt0, wt1), (gm0, gm1), (hh0, hh1)
+
+    row = lax.broadcasted_iota(jnp.int32, (wide, PIX), 0) // 8
+    part = jnp.where(row < 18, row % 6, 6)
+    mono[...] = monomials(part, lax.broadcasted_iota(jnp.int32, (wide, PIX), 1)).astype(BF16)
+    part = lax.broadcasted_iota(jnp.int32, (16, PIX), 0)
+    mono_t[...] = monomials(part, lax.broadcasted_iota(jnp.int32, (16, PIX), 1)).astype(BF16)
 
     def place(group, k, t):
         return (group * kmax + k) * 8 + t
@@ -293,7 +312,7 @@
             mid_y = ((tile_id // TILE_COLS) * 16 + 8).astype(F32)
             shift = jnp.where(rows16 == 0, mid_x, jnp.where(rows16 == 1, mid_y, 0.0))
             for k in range(kmax):
-                slot = slots[tile, k]
+                slot = slots[k, tile]
                 base = jnp.maximum(slot, 0) * FEAT
                 spot = place(group, k, t) * 16
                 raw[spot : spot + FEAT, :] = in_ref[pl.ds(base, FEAT), :] - shift[0:FEAT]
@@ -316,32 +335,36 @@
         poly_b,
         poly_c,
     ]
-    mat[...] = jnp.zeros(mat.shape, F32)
+    blank = jnp.zeros((8, G), F32)
+    rows_of = [blank] * ROWS
     for index in range(6):
-        mat[pl.ds(index, picks, stride=16), :] = coefs[index]
+        for piece, value in enumerate(pieces3(coefs[index])):
+            rows_of[6 * piece + index] = value
+    mat_c[...] = jnp.zeros(mat_c.shape, F32)
     for channel in range(3):
-        mat[pl.ds(8 + channel, picks, stride=16), :] = feature(6 + channel)
-    whole = mat[...]
-    high, low = split2(whole)
-    mat_h[...] = high
-    mat_m[...] = low
-
-    for group in range(groups):
-        for k in range(kmax):
-            chunk = group * kmax + k
-            turned = mat[chunk * G : (chunk + 1) * G, :].T
-            first = turned.astype(BF16)
-            rest = turned - first.astype(F32)
-            second = rest.astype(BF16)
-            third = (rest - second.astype(F32)).astype(BF16)
-            trio = jnp.concatenate([first, second, third], axis=1)
-            left[chunk * G : (chunk + 1) * G, :] = trio
-            lanes3 = lax.broadcasted_iota(jnp.int32, (1, 3 * G), 1) % G
-            for t in range(8):
-                mask = jnp.where(lanes3 // 16 == t, 1.0, 0.0).astype(BF16)
-                alpha = jnp.exp2(dot(trio * mask, mono[...]))
-                for half in range(2):
-                    alphas[half][pl.ds(chunk * G * 8 + t, G, stride=8), :] = alpha[:, half * G : (half + 1) * G]
+        high, middle, _ = pieces3(feature(6 + channel))
+        rows_of[18 + channel] = high
+        rows_of[21 + channel] = middle
+        rows_of[24 + channel] = high
+        mat_c[pl.ds(channel, picks, stride=16), :] = high
+        mat_c[pl.ds(3 + channel, picks, stride=16), :] = middle
+    for chunk in range(groups * kmax):
+        for index, value in enumerate(rows_of):
+            start = chunk * wide + index * 8
+            mat[start : start + 8, :] = value if index >= 27 else value[chunk * 8 : chunk * 8 + 8]
+    mat_b[...] = mat_c[...].astype(BF16)
+
+    lane_tile = lax.broadcasted_iota(jnp.int32, (1, wide), 1) % 8
+    masks = [jnp.where(lane_tile == t, 1.0, 0.0).astype(BF16) for t in range(8)]
+
+    for chunk in range(groups * kmax):
+        sides = [mat[chunk * wide + half * G : chunk * wide + (half + 1) * G, :].T for half in range(2)]
+        turned = jnp.concatenate(sides, axis=1).astype(BF16)
+        left[chunk * G : (chunk + 1) * G, :] = turned
+        for t in range(8):
+            alpha = jnp.exp2(dot(turned * masks[t], mono[...]))
+            for half in range(2):
+                alphas[half][pl.ds(chunk * G * 8 + t, G, stride=8), :] = alpha[:, half * G : (half + 1) * G]
 
     count = kmax * G
 
@@ -351,9 +374,9 @@
             row = pl.multiple_of((group * count + step) * 8, 8)
             for half in range(2):
                 at = group * 2 + half
-                weight = keeps[at] * alphas[half][pl.ds(row, 8), :]
-                weights[half][pl.ds(row, 8), :] = weight
-                keeps[at] = keeps[at] - weight
+                alpha = alphas[half][pl.ds(row, 8), :]
+                weights[half][pl.ds(row, 8), :] = keeps[at] * alpha
+                keeps[at] = keeps[at] * (1.0 - alpha)
         return tuple(keeps)
 
     ones = jnp.ones((8, G), F32)
@@ -369,13 +392,11 @@
                 w_high, w_low = split2(weight)
                 wt_h[spot * G : (spot + 1) * G, :] = w_high
                 wt_l[spot * G : (spot + 1) * G, :] = w_low
-                m_high = mat_h[spot * 16 : spot * 16 + 16, :]
-                m_low = mat_m[spot * 16 : spot * 16 + 16, :]
-                both = dot(jnp.concatenate([m_high, m_low], axis=0), w_high)
-                total = total + both[0:16] + both[16:32] + dot(m_high, w_low)
+                own = mat_b[spot * 16 : (spot + 1) * 16, :]
+                total = total + dot(own, w_high) + dot(own, w_low)
             for channel in range(3):
                 row = channel * tiles + group * 8 + t
-                ccol[row : row + 1, :] = total[8 + channel : 9 + channel, :]
+                ccol[row : row + 1, :] = total[channel : channel + 1, :] + total[3 + channel : 4 + channel, :]
 
     colour = [ccol[c * tiles : (c + 1) * tiles, :] for c in range(3)]
     miss = []
@@ -383,8 +404,8 @@
         value = colour[i] + expo[0, 9 + i]
         for j in range(3):
             value = value + expo[0, 3 * i + j] * colour[j]
-        shown_ref[:, i, :] = value
-        miss.append(value - goal_ref[:, i, :])
+        shown_ref[i] = value
+        miss.append(value - goal_ref[i])
     slope = []
     for j in range(3):
         value = miss[j]
@@ -397,80 +418,64 @@
         folded = jnp.sum(value[:, 0:G] + value[:, G : 2 * G], axis=0, keepdims=True)
         expo_row = jnp.where(lanes == index, jnp.sum(folded, axis=1, keepdims=True), expo_row)
 
+    highs = [value.astype(BF16).astype(F32) for value in slope]
+    lows = [value - high for value, high in zip(slope, highs)]
     for group in range(groups):
-        base = group * 3 * G
-        for half in range(2):
-            side = slice(half * G, (half + 1) * G)
-            highs, lows = [], []
-            for channel in range(3):
-                value = slope[channel][group * 8 : group * 8 + 8, side]
-                s_high = value.astype(BF16).astype(F32)
-                highs.append(s_high)
-                lows.append(value - s_high)
-            gall[...] = jnp.zeros(gall.shape, F32)
-            for channel in range(3):
-                gall[pl.ds(8 + channel, 8, stride=16), :] = lows[channel]
-            gsplit[base + 2 * G : base + 3 * G, side] = gall[...].astype(BF16)
-            for channel in range(3):
-                gall[pl.ds(8 + channel, 8, stride=16), :] = highs[channel]
-            g_high = gall[...].astype(BF16)
-            gsplit[base : base + G, side] = g_high
-            gsplit[base + G : base + 2 * G, side] = g_high
-            for channel in range(3):
-                gall[pl.ds(11 + channel, 8, stride=16), :] = lows[channel]
-            turned = gall[...].T.astype(BF16)
-            start = group * 2 * PIX + half * G
-            gtr[start : start + G, :] = turned
-            gtr[start + PIX : start + PIX + G, :] = turned
-        g_rhs = gsplit[base : base + 3 * G, :]
-        for k in range(kmax):
-            chunk = group * kmax + k
-            first = left[chunk * G : (chunk + 1) * G, 0:G]
-            second = left[chunk * G : (chunk + 1) * G, G : 2 * G]
-            trio = jnp.concatenate([first, second, first], axis=1)
-            lanes3 = lax.broadcasted_iota(jnp.int32, (1, 3 * G), 1) % G
-            for t in range(8):
-                mask = jnp.where(lanes3 // 16 == t, 1.0, 0.0).astype(BF16)
-                value = dot(trio * mask, g_rhs)
-                for half in range(2):
-                    slopes[half][pl.ds(chunk * G * 8 + t, G, stride=8), :] = value[:, half * G : (half + 1) * G]
+        span = slice(group * 8, group * 8 + 8)
+        nine = [value[span] for value in highs + highs + lows]
+        stack = [jnp.zeros((18 * 8, PIX), F32)] + nine + [jnp.zeros(((ROWS - 27) * 8, PIX), F32)]
+        g_rhs[group * wide : (group + 1) * wide, :] = jnp.concatenate(stack, axis=0).astype(BF16)
+    gall[...] = jnp.zeros(gall.shape, F32)
+    for half in range(2):
+        side = slice(half * G, (half + 1) * G)
+        for channel in range(3):
+            gall[pl.ds(channel, tiles, stride=16), :] = highs[channel][:, side]
+            gall[pl.ds(3 + channel, tiles, stride=16), :] = lows[channel][:, side]
+        g_own[:, side] = gall[...].astype(BF16)
+    for chunk in range(groups * kmax):
+        turned = left[chunk * G : (chunk + 1) * G, :]
+        group = chunk // kmax
+        right = g_rhs[group * wide : (group + 1) * wide, :]
+        for t in range(8):
+            value = dot(turned * masks[t], right)
+            for half in range(2):
+                slopes[half][pl.ds(chunk * G * 8 + t, G, stride=8), :] = value[:, half * G : (half + 1) * G]
+
+    batch = 8
 
     def backward(step, behind):
         behind = list(behind)
-        for group in range(groups):
-            row = pl.multiple_of((group * count + (count - 1 - step)) * 8, 8)
-            for half in range(2):
-                at = group * 2 + half
-                gap = slopes[half][pl.ds(row, 8), :] - behind[at]
-                slopes[half][pl.ds(row, 8), :] = weights[half][pl.ds(row, 8), :] * gap
-                behind[at] = behind[at] + alphas[half][pl.ds(row, 8), :] * gap
+        base = pl.multiple_of((count - batch - step * batch) * 8, 8 * batch)
+        for inner in range(batch - 1, -1, -1):
+            for group in range(groups):
+                rows = pl.ds(base + (group * count + inner) * 8, 8)
+                for half in range(2):
+                    at = group * 2 + half
+                    alpha = alphas[half][rows, :]
+                    value = slopes[half][rows, :]
+                    moved[half][rows, :] = weights[half][rows, :] * (value - behind[at])
+                    behind[at] = behind[at] * (1.0 - alpha) + alpha * value
         return tuple(behind)
 
     zeros = jnp.zeros((8, G), F32)
-    lax.fori_loop(0, count, backward, (zeros,) * (2 * groups), unroll=8)
-
-    lane_tile = lax.broadcasted_iota(jnp.int32, (G, G), 1) // 16
+    lax.fori_loop(0, count // batch, backward, (zeros,) * (2 * groups))
+
     for group in range(groups):
-        g_t = gtr[group * 2 * PIX : (group + 1) * 2 * PIX, :]
         for k in range(kmax):
-            chunk = group * kmax + k
-            acc = jnp.zeros((G, G), F32)
             for t in range(8):
                 spot = place(group, k, t)
-                rows = pl.ds(chunk * G * 8 + t, G, stride=8)
-                value = jnp.concatenate([slopes[0][rows, :], slopes[1][rows, :]], axis=1)
+                rows = pl.ds((group * kmax + k) * G * 8 + t, G, stride=8)
+                value = jnp.concatenate([moved[0][rows, :].T, moved[1][rows, :].T], axis=0)
                 v_high, v_low = split2(value)
-                out = dot(jnp.concatenate([v_high, v_low], axis=1), mono_t[...])
+                table = mono_t[...]
+                sums = dot(table, v_high) + dot(table, v_low)
+                mom[spot * 8 : (spot + 1) * 8, :] = sums[0:8]
+                own = g_own[(group * 8 + t) * 16 : (group * 8 + t + 1) * 16, :]
                 w_high = wt_h[spot * G : (spot + 1) * G, :]
                 w_low = wt_l[spot * G : (spot + 1) * G, :]
-                out = out + dot(jnp.concatenate([w_high, w_low], axis=1), g_t)
-                acc = jnp.where(lane_tile == t, out, acc)
-            mat[chunk * G : (chunk + 1) * G, :] = acc.T
-
-    def moment(index):
-        return mat[pl.ds(index, picks, stride=16), :]
-
-    sum_0, sum_x, sum_y, sum_xx, sum_xy, sum_yy = [moment(i) for i in range(6)]
+                mat_c[spot * 16 : (spot + 1) * 16, :] = dot_t(own, w_high) + dot_t(own, w_low)
+
+    sum_0, sum_x, sum_y, sum_xx, sum_xy, sum_yy = [mom[pl.ds(i, picks, stride=8), :] for i in range(6)]
     off_x, off_y, con_a, con_b, con_c, opac = [feature(i) for i in range(6)]
     cen_x = sum_x - off_x * sum_0
     cen_y = sum_y - off_y * sum_0
@@ -484,7 +489,11 @@
         -cen_xy,
         -0.5 * cen_yy,
         sum_0 / opac,
-    ] + [moment(8 + c) + moment(11 + c) for c in range(3)]
+    ]
+    for channel in range(3):
+        outs.append(
+            mat_c[pl.ds(channel, picks, stride=16), :] + mat_c[pl.ds(3 + channel, picks, stride=16), :]
+        )
     for index, value in enumerate(outs):
         raw[pl.ds(index, picks, stride=16), :] = value
 
@@ -492,7 +501,7 @@
     for group in range(groups):
         for k in range(kmax):
             for t in range(8):
-                slot = jnp.maximum(slots[group * 8 + t, k], 0)
+                slot = jnp.maximum(slots[k, group * 8 + t], 0)
                 where = pl.ds((slot // cap) * stride + (slot % cap) * FEAT, FEAT)
                 spot = place(group, k, t) * 16
                 grad_ref[where, :] = grad_ref[where, :] + raw[spot : spot + FEAT, :]
@@ -513,8 +522,12 @@
     return moved.reshape(rows.shape)
 
 
+def near(rows):
+    return pltpu.with_memory_space_constraint(rows, pltpu.VMEM)
+
+
 def render(tile_ids, slots, expo, incoming, goal, interpret=False):
-    tiles, kmax = slots.shape
+    kmax, tiles = slots.shape
     picks = tiles * kmax
     groups = tiles // 8
     scene = incoming.shape[0] // (2 * FEAT)
@@ -522,19 +535,21 @@
     return pl.pallas_call(
         render_kernel,
         out_shape=(
-            jax.ShapeDtypeStruct((tiles, 3, PIX), F32),
-            jax.ShapeDtypeStruct((scene * (2 * FEAT + 1), G), F32),
+            jax.ShapeDtypeStruct((3, tiles, PIX), F32),
+            pltpu.VMEM((scene * (2 * FEAT + 1), G), F32),
         ),
         in_specs=[smem(), smem(), smem(), vmem(), vmem()],
         out_specs=(vmem(), vmem()),
         scratch_shapes=[
             pltpu.VMEM((picks * 16, G), F32),
+            pltpu.VMEM((picks * ROWS, G), F32),
             pltpu.VMEM((picks * 16, G), F32),
             pltpu.VMEM((picks * 16, G), BF16),
-            pltpu.VMEM((picks * 16, G), BF16),
-            pltpu.VMEM((groups * kmax * G, 3 * G), BF16),
-            pltpu.VMEM((3 * G, PIX), BF16),
-            pltpu.VMEM((2 * PIX, G), BF16),
+            pltpu.VMEM((groups * kmax * G, 8 * ROWS), BF16),
+            pltpu.VMEM((8 * ROWS, PIX), BF16),
+            pltpu.VMEM((16, PIX), BF16),
+            big,
+            big,
             big,
             big,
             big,
@@ -544,9 +559,10 @@
             pltpu.VMEM((picks * G, PIX), BF16),
             pltpu.VMEM((picks * G, PIX), BF16),
             pltpu.VMEM((3 * tiles, PIX), F32),
-            pltpu.VMEM((G, G), F32),
-            pltpu.VMEM((groups * 3 * G, PIX), BF16),
-            pltpu.VMEM((groups * 2 * PIX, G), BF16),
+            pltpu.VMEM((tiles * 16, G), F32),
+            pltpu.VMEM((tiles * ROWS, PIX), BF16),
+            pltpu.VMEM((tiles * 16, PIX), BF16),
+            pltpu.VMEM((picks * 8, G), F32),
         ],
         compiler_params=pltpu.CompilerParams(vmem_limit_bytes=56 * 1024 * 1024),
         name="render",
@@ -571,12 +587,18 @@
     scene = lax.axis_size("scene")
     blocks = means.shape[0]
     cap = send_list.shape[3]
-    pieces = (means, log_scales, rotations, opacity_logits, colour_coefs)
-    picks = send_list[0, 0]
-    own_rows = jax.ShapeDtypeStruct((views * blocks * FEAT, G), F32)
+    pieces = (
+        means.transpose(1, 0, 2),
+        log_scales.transpose(1, 0, 2),
+        rotations,
+        opacity_logits,
+        colour_coefs,
+    )
+    picks = send_list[0, 0].T
+    own_count = views * blocks * FEAT
     own_proj = pl.pallas_call(
         project_kernel,
-        out_shape=own_rows,
+        out_shape=pltpu.VMEM((own_count, G), F32),
         in_specs=[vmem()] * 6,
         out_specs=vmem(),
         name="project",
@@ -584,21 +606,23 @@
     projected = across(own_proj, "view", views)
     outgoing = pl.pallas_call(
         gather_kernel,
-        out_shape=jax.ShapeDtypeStruct((scene * cap * FEAT, G), F32),
+        out_shape=pltpu.VMEM((scene * cap * FEAT, G), F32),
         in_specs=[smem(), vmem()],
         out_specs=vmem(),
         name="gather",
-    )(picks, projected)
+    )(picks, near(projected))
     incoming = across(outgoing, "scene", scene)
-    shown, grad_rows = render(tile_ids[0], pair_slots[0], exposure, incoming, target[0])
+    shown, grad_rows = render(
+        tile_ids[0], pair_slots[0].T, exposure, near(incoming), target[0].transpose(1, 0, 2)
+    )
     returned = across(grad_rows, "scene", scene)
     grad_proj, grad_expo = pl.pallas_call(
         scatter_kernel,
-        out_shape=(own_rows, jax.ShapeDtypeStruct((1, 12), F32)),
+        out_shape=(pltpu.VMEM((own_count, G), F32), jax.ShapeDtypeStruct((1, 12), F32)),
         in_specs=[smem(), vmem()],
         out_specs=(vmem(), vmem()),
         name="scatter",
-    )(picks, returned)
+    )(picks, near(returned))
     sent_back = across(grad_proj, "view", views)
     grads = pl.pallas_call(
         unproject_kernel,
@@ -606,8 +630,17 @@
         in_specs=[vmem()] * 7,
         out_specs=tuple(vmem() for _ in pieces),
         name="unproject",
-    )(*pieces, cameras, sent_back)
-    return (shown[None], *grads, grad_expo)
+    )(*pieces, cameras, near(sent_back))
+    g_means, g_scales, g_rot, g_logits, g_coefs = grads
+    return (
+        shown.transpose(1, 0, 2)[None],
+        g_means.transpose(1, 0, 2),
+        g_scales.transpose(1, 0, 2),
+        g_rot,
+        g_logits,
+        g_coefs,
+        grad_expo,
+    )
 
 
 def solution(mesh):

time: 153 us -> 134 us (0.88)
  blocking collectives: 42.2 us -> 113 us
  waiting for transfers between devices: 38.3 us -> 0 us
  starting transfers between devices: 31.4 us -> 0 us
  Pallas kernels: 30.5 us -> 19.6 us
  local copies, waits for them, and re-layouts: 9.16 us -> 0 us
    all_to_all x1 -> x4, blocking collectives: 42.2 us -> 113 us  [across(): lax.all_to_all(shaped, axis, split_axis=0, concat_axis=0, tiled=True)]
    all_to_all x3 -> x0, waiting for transfers between devices: 38.3 us -> none  [across(): lax.all_to_all(shaped, axis, split_axis=0, concat_axis=0, tiled=True)]
    all_to_all x3 -> x0, starting transfers between devices: 31.4 us -> none  [across(): lax.all_to_all(shaped, axis, split_axis=0, concat_axis=0, tiled=True)]
    pallas_call x4, Pallas kernels: 28.4 us -> 17.7 us  [the longest x1 14 us: render(): pl.pallas_call(render_kernel, out_shape=(jax.ShapeDtypeStruct((3, tiles,...]
    unnamed x24 -> x0, local copies, waits for them, and re-layouts: 7.77 us -> none
  transfers between devices with their start and end apart: 3 -> 0, of which waited for: 3 -> 0; matrix products, arithmetic and copies ran while one was open for 2% -> 0% of each run, Pallas kernels for 0% -> 0%
where the time goes in v2:
time: 134 us
  blocking collectives  113 us (84%)
  Pallas kernels  19.6 us (15%)
    all_to_all x4, blocking collectives, across(): lax.all_to_all(shaped, axis, split_axis=0, concat_axis=0, tiled=True)  113 us
    pallas_call x1, Pallas kernels, render(): pl.pallas_call(render_kernel, out_shape=(jax.ShapeDtypeStruct((3, tiles,...  14 us

profile of v2, /device:TPU:1, one launch (start us, length us, event | category | flops | bytes accessed | tf_op | source)
XLA Modules:
  0.0 133.7 jit_solution(15724031195408436384)
XLA Ops:
  0.6 1.0 project.1
  1.7 14.1 %all_to_all.20 = f32[8,18,1,128]{3,2,1,0:T(1,128)S(1)} all-to-all(f32[8,18,1,128]{3,2,1,0:T(1,128)S(1)} %bitcast.30), channel_id=1, replica_groups=mesh['view'=8,'scene'=64] {'view'}, dimensions={0} | all-to-all | bytes 147456 | tf_op jit(solution)/shard_map/all_to_all | solution.py:521
  15.8 0.9 gather.1
  16.7 46.5 %all_to_all.21 = f32[64,18,1,128]{3,2,1,0:T(1,128)S(1)} all-to-all(f32[64,18,1,128]{3,2,1,0:T(1,128)S(1)} %bitcast.27), channel_id=1, replica_groups=mesh['view'=8,'scene'=64] {'scene'}, dimensions={0} | all-to-all | bytes 1179648 | tf_op jit(solution)/shard_map/all_to_all | solution.py:521
  63.2 14.0 %render.1 = (f32[3,16,256]{2,1,0:T(8,128)}, f32[1216,128]{1,0:T(8,128)S(1)}) custom-call(s32[16]{0:T(128)} %bitcast.41, s32[4,16]{1,0:T(4,128)} %bitcast.40, f32[1,12]{1,0:T(1,128)} %expo.1, f32[1152,128]{1,0:T(8,128)S(1)} %bitcast.26, f32[3,16,256]{2,1,0:T(8,128)} %bitcast.33), custom_call_target="tpu_custom_call" | custom-call | tf_op jit(solution)/shard_map/render/pallas_call | solution.py:535
  77.2 41.9 %all_to_all.22 = f32[64,19,1,128]{3,2,1,0:T(1,128)S(1)} all-to-all(f32[64,19,1,128]{3,2,1,0:T(1,128)S(1)} %bitcast.28), channel_id=1, replica_groups=mesh['view'=8,'scene'=64] {'scene'}, dimensions={0} | all-to-all | bytes 1245184 | tf_op jit(solution)/shard_map/all_to_all | solution.py:521
  119.1 1.8 %scatter.1 = (f32[144,128]{1,0:T(8,128)S(1)}, f32[1,12]{1,0:T(1,128)}) custom-call(s32[2,64]{1,0:T(2,128)} %bitcast.39, f32[1216,128]{1,0:T(8,128)S(1)} %bitcast.25), custom_call_target="tpu_custom_call" | custom-call | tf_op jit(solution)/shard_map/scatter/pallas_call | solution.py:619
  120.8 11.0 %all_to_all.23 = f32[8,18,1,128]{3,2,1,0:T(1,128)S(1)} all-to-all(f32[8,18,1,128]{3,2,1,0:T(1,128)S(1)} %bitcast.32), channel_id=1, replica_groups=mesh['view'=8,'scene'=64] {'view'}, dimensions={0} | all-to-all | bytes 147456 | tf_op jit(solution)/shard_map/all_to_all | solution.py:521
  131.8 1.9 %unproject.1 = (f32[3,2,128]{2,1,0:T(2,128)}, f32[3,2,128]{2,1,0:T(2,128)}, f32[2,4,128]{2,1,0:T(4,128)}, f32[2,1,128]{2,1,0:T(1,128)}, f32[2,48,128]{2,1,0:T(8,128)}) custom-call(f32[3,2,128]{2,1,0:T(2,128)} %bitcast.35, f32[3,2,128]{2,1,0:T(2,128)} %bitcast.37, f32[2,4,128]{2,1,0:T(4,128)} %rotations.3, f32[2,1,128]{2,1,0:T(1,128)} %logits.3, ...), custom_call_target="tpu_custom_call" | custom-call | tf_op jit(solution)/shard_map/unproject/pallas_call | solution.py:627

commit v3 on v2

--- a/solution.py
+++ b/solution.py
@@ -145,16 +145,15 @@
     ] + colours
 
 
-def block_inputs(refs, block, views):
-    means, log_scales, rotations, logits, coefs = refs
-
-    def rows(ref, count):
-        return [jnp.broadcast_to(ref[block, pl.ds(r, 1), :], (views, G)) for r in range(count)]
-
-    def turned(ref):
-        return [jnp.broadcast_to(ref[r, pl.ds(block, 1), :], (views, G)) for r in range(3)]
-
-    return (turned(means), turned(log_scales), rows(rotations, 4), rows(logits, 1)[0], rows(coefs, 48))
+KEPT = 64
+
+
+def block_inputs(kept, block, views):
+    def rows(first, count):
+        start = block * KEPT + first
+        return [jnp.broadcast_to(kept[start + r : start + r + 1, :], (views, G)) for r in range(count)]
+
+    return (rows(0, 3), rows(3, 3), rows(6, 4), rows(10, 1)[0], rows(16, 48))
 
 
 def camera_columns(cam_ref, views):
@@ -162,28 +161,37 @@
     return [jnp.broadcast_to(cams[:, col : col + 1], (views, G)) for col in range(16)]
 
 
-def project_kernel(means, log_scales, rotations, logits, coefs, cam_ref, out_ref):
-    views = cam_ref.shape[0]
-    blocks = rotations.shape[0]
-    cam = camera_columns(cam_ref, views)
-    for block in range(blocks):
-        pieces = block_inputs((means, log_scales, rotations, logits, coefs), block, views)
-        for feat, value in enumerate(project(*pieces, cam)):
-            out_ref[pl.ds(block * FEAT + feat, views, stride=blocks * FEAT), :] = value
-
-
-def unproject_kernel(
-    means, log_scales, rotations, logits, coefs, cam_ref, back_ref, o_means, o_scales, o_rot, o_logit, o_coef
+def project_kernel(
+    means, log_scales, rotations, logits, coefs, cam_ref, picks, out_ref, kept, cam_kept, picks_kept
 ):
     views = cam_ref.shape[0]
     blocks = rotations.shape[0]
+    cam_kept[...] = cam_ref[...]
+    picks_kept[...] = picks[...]
+    cam = camera_columns(cam_ref, views)
+    for block in range(blocks):
+        start = block * KEPT
+        for r in range(3):
+            kept[start + r : start + r + 1, :] = means[r, pl.ds(block, 1), :]
+            kept[start + 3 + r : start + 4 + r, :] = log_scales[r, pl.ds(block, 1), :]
+        kept[start + 6 : start + 10, :] = rotations[block]
+        kept[start + 10 : start + 11, :] = logits[block]
+        kept[start + 11 : start + 16, :] = jnp.zeros((5, G), F32)
+        kept[start + 16 : start + KEPT, :] = coefs[block]
+        for feat, value in enumerate(project(*block_inputs(kept, block, views), cam)):
+            out_ref[pl.ds(block * FEAT + feat, views, stride=blocks * FEAT), :] = value
+
+
+def unproject_kernel(kept, cam_ref, back_ref, o_means, o_scales, o_rot, o_logit, o_coef):
+    views = cam_ref.shape[0]
+    blocks = o_rot.shape[0]
     cam = camera_columns(cam_ref, views)
 
     def total(value):
         return jnp.sum(value, axis=0, keepdims=True)
 
     for block in range(blocks):
-        pieces = block_inputs((means, log_scales, rotations, logits, coefs), block, views)
+        pieces = block_inputs(kept, block, views)
         _, pull = jax.vjp(lambda *own: project(*own, cam), *pieces)
         seeds = [
             back_ref[pl.ds(block * FEAT + feat, views, stride=blocks * FEAT), :] for feat in range(FEAT)
@@ -197,23 +205,34 @@
                 ref[block, pl.ds(row, 1), :] = total(value)
 
 
+def chosen(picks, cap, blocks):
+    spots = lax.broadcasted_iota(jnp.int32, (blocks, picks.shape[1]), 0)
+    return [jnp.where(spots == picks[c : c + 1, :], 1.0, 0.0) for c in range(cap)]
+
+
 def gather_kernel(picks, src_ref, out_ref):
     cap, renderers = picks.shape
-    for r in range(renderers):
+    blocks = src_ref.shape[0] // FEAT
+    turned = [select.T.astype(BF16) for select in chosen(jnp.maximum(picks[...], 0), cap, blocks)]
+    for feat in range(FEAT):
+        pieces = [piece.astype(BF16) for piece in pieces3(src_ref[pl.ds(feat, blocks, stride=FEAT), :])]
         for c in range(cap):
-            pick = jnp.maximum(picks[c, r], 0)
-            out_ref[pl.ds((r * cap + c) * FEAT, FEAT), :] = src_ref[pl.ds(pick * FEAT, FEAT), :]
+            value = dot(turned[c], pieces[0]) + dot(turned[c], pieces[1]) + dot(turned[c], pieces[2])
+            out_ref[pl.ds(c * FEAT + feat, renderers, stride=cap * FEAT), :] = value
 
 
 def scatter_kernel(picks, src_ref, out_ref, expo_ref):
     cap, renderers = picks.shape
     stride = cap * FEAT + 1
-    out_ref[...] = jnp.zeros(out_ref.shape, F32)
-    for r in range(renderers):
+    blocks = out_ref.shape[0] // FEAT
+    selects = [select.astype(BF16) for select in chosen(picks[...], cap, blocks)]
+    for feat in range(FEAT):
+        total = jnp.zeros((blocks, G), F32)
         for c in range(cap):
-            pick = jnp.maximum(picks[c, r], 0)
-            place = pl.ds(pick * FEAT, FEAT)
-            out_ref[place, :] = out_ref[place, :] + src_ref[pl.ds(r * stride + c * FEAT, FEAT), :]
+            rows = src_ref[pl.ds(c * FEAT + feat, renderers, stride=stride), :]
+            for piece in pieces3(rows):
+                total = total + dot(selects[c], piece.astype(BF16))
+        out_ref[pl.ds(feat, blocks, stride=FEAT), :] = total
     terms = src_ref[pl.ds(stride - 1, renderers, stride=stride), :]
     expo_ref[...] = jnp.sum(terms, axis=0, keepdims=True)[:, 0:12]
 
@@ -251,6 +270,7 @@
 
 
 ROWS = 32
+PITCH = 9
 
 
 def render_kernel(
@@ -364,36 +384,41 @@
         for t in range(8):
             alpha = jnp.exp2(dot(turned * masks[t], mono[...]))
             for half in range(2):
-                alphas[half][pl.ds(chunk * G * 8 + t, G, stride=8), :] = alpha[:, half * G : (half + 1) * G]
+                alphas[half][pl.ds(chunk * G * PITCH + t, G, stride=PITCH), :] = alpha[:, half * G : (half + 1) * G]
 
     count = kmax * G
+
+    batch = 8
 
     def forward(step, keeps):
         keeps = list(keeps)
-        for group in range(groups):
-            row = pl.multiple_of((group * count + step) * 8, 8)
-            for half in range(2):
-                at = group * 2 + half
-                alpha = alphas[half][pl.ds(row, 8), :]
-                weights[half][pl.ds(row, 8), :] = keeps[at] * alpha
-                keeps[at] = keeps[at] * (1.0 - alpha)
+        base = step * (batch * PITCH)
+        for inner in range(batch):
+            for group in range(groups):
+                rows = pl.ds(base + (group * count + inner) * PITCH, 8)
+                for half in range(2):
+                    at = group * 2 + half
+                    alpha = alphas[half][rows, :]
+                    weights[half][rows, :] = keeps[at] * alpha
+                    keeps[at] = keeps[at] * (1.0 - alpha)
         return tuple(keeps)
 
     ones = jnp.ones((8, G), F32)
-    lax.fori_loop(0, count, forward, (ones,) * (2 * groups), unroll=8)
+    lax.fori_loop(0, count // batch, forward, (ones,) * (2 * groups))
 
     for group in range(groups):
         for t in range(8):
             total = jnp.zeros((16, PIX), F32)
             for k in range(kmax):
                 spot = place(group, k, t)
-                rows = pl.ds((group * kmax + k) * G * 8 + t, G, stride=8)
+                rows = pl.ds((group * kmax + k) * G * PITCH + t, G, stride=PITCH)
                 weight = jnp.concatenate([weights[0][rows, :], weights[1][rows, :]], axis=1)
                 w_high, w_low = split2(weight)
                 wt_h[spot * G : (spot + 1) * G, :] = w_high
                 wt_l[spot * G : (spot + 1) * G, :] = w_low
                 own = mat_b[spot * 16 : (spot + 1) * 16, :]
-                total = total + dot(own, w_high) + dot(own, w_low)
+                total = total + dot(own, wt_h[spot * G : (spot + 1) * G, :])
+                total = total + dot(own, wt_l[spot * G : (spot + 1) * G, :])
             for channel in range(3):
                 row = channel * tiles + group * 8 + t
                 ccol[row : row + 1, :] = total[channel : channel + 1, :] + total[3 + channel : 4 + channel, :]
@@ -439,16 +464,14 @@
         for t in range(8):
             value = dot(turned * masks[t], right)
             for half in range(2):
-                slopes[half][pl.ds(chunk * G * 8 + t, G, stride=8), :] = value[:, half * G : (half + 1) * G]
-
-    batch = 8
+                slopes[half][pl.ds(chunk * G * PITCH + t, G, stride=PITCH), :] = value[:, half * G : (half + 1) * G]
 
     def backward(step, behind):
         behind = list(behind)
-        base = pl.multiple_of((count - batch - step * batch) * 8, 8 * batch)
+        base = (count - batch - step * batch) * PITCH
         for inner in range(batch - 1, -1, -1):
             for group in range(groups):
-                rows = pl.ds(base + (group * count + inner) * 8, 8)
+                rows = pl.ds(base + (group * count + inner) * PITCH, 8)
                 for half in range(2):
                     at = group * 2 + half
                     alpha = alphas[half][rows, :]
@@ -464,18 +487,18 @@
         for k in range(kmax):
             for t in range(8):
                 spot = place(group, k, t)
-                rows = pl.ds((group * kmax + k) * G * 8 + t, G, stride=8)
+                rows = pl.ds((group * kmax + k) * G * PITCH + t, G, stride=PITCH)
                 value = jnp.concatenate([moved[0][rows, :].T, moved[1][rows, :].T], axis=0)
                 v_high, v_low = split2(value)
                 table = mono_t[...]
                 sums = dot(table, v_high) + dot(table, v_low)
-                mom[spot * 8 : (spot + 1) * 8, :] = sums[0:8]
+                mom[spot * PITCH : spot * PITCH + 8, :] = sums[0:8]
                 own = g_own[(group * 8 + t) * 16 : (group * 8 + t + 1) * 16, :]
                 w_high = wt_h[spot * G : (spot + 1) * G, :]
                 w_low = wt_l[spot * G : (spot + 1) * G, :]
                 mat_c[spot * 16 : (spot + 1) * 16, :] = dot_t(own, w_high) + dot_t(own, w_low)
 
-    sum_0, sum_x, sum_y, sum_xx, sum_xy, sum_yy = [mom[pl.ds(i, picks, stride=8), :] for i in range(6)]
+    sum_0, sum_x, sum_y, sum_xx, sum_xy, sum_yy = [mom[pl.ds(i, picks, stride=PITCH), :] for i in range(6)]
     off_x, off_y, con_a, con_b, con_c, opac = [feature(i) for i in range(6)]
     cen_x = sum_x - off_x * sum_0
     cen_y = sum_y - off_y * sum_0
@@ -531,7 +554,7 @@
     picks = tiles * kmax
     groups = tiles // 8
     scene = incoming.shape[0] // (2 * FEAT)
-    big = pltpu.VMEM((picks * G, G), F32)
+    big = pltpu.VMEM((picks // 8 * G * PITCH, G), F32)
     return pl.pallas_call(
         render_kernel,
         out_shape=(
@@ -562,7 +585,7 @@
             pltpu.VMEM((tiles * 16, G), F32),
             pltpu.VMEM((tiles * ROWS, PIX), BF16),
             pltpu.VMEM((tiles * 16, PIX), BF16),
-            pltpu.VMEM((picks * 8, G), F32),
+            pltpu.VMEM((picks * PITCH, G), F32),
         ],
         compiler_params=pltpu.CompilerParams(vmem_limit_bytes=56 * 1024 * 1024),
         name="render",
@@ -596,41 +619,46 @@
     )
     picks = send_list[0, 0].T
     own_count = views * blocks * FEAT
-    own_proj = pl.pallas_call(
+    own_proj, kept, cams, picks = pl.pallas_call(
         project_kernel,
-        out_shape=pltpu.VMEM((own_count, G), F32),
-        in_specs=[vmem()] * 6,
-        out_specs=vmem(),
+        out_shape=(
+            pltpu.VMEM((own_count, G), F32),
+            pltpu.VMEM((blocks * KEPT, G), F32),
+            pltpu.VMEM(cameras.shape, F32),
+            pltpu.VMEM(picks.shape, picks.dtype),
+        ),
+        in_specs=[vmem()] * 7,
+        out_specs=(vmem(),) * 4,
         name="project",
-    )(*pieces, cameras)
+    )(*pieces, cameras, picks)
     projected = across(own_proj, "view", views)
     outgoing = pl.pallas_call(
         gather_kernel,
         out_shape=pltpu.VMEM((scene * cap * FEAT, G), F32),
-        in_specs=[smem(), vmem()],
+        in_specs=[vmem(), vmem()],
         out_specs=vmem(),
         name="gather",
-    )(picks, near(projected))
+    )(near(picks), near(projected))
     incoming = across(outgoing, "scene", scene)
     shown, grad_rows = render(
-        tile_ids[0], pair_slots[0].T, exposure, near(incoming), target[0].transpose(1, 0, 2)
+        tile_ids[0], pair_slots[0].T, exposure, near(incoming), near(target[0].transpose(1, 0, 2))
     )
     returned = across(grad_rows, "scene", scene)
     grad_proj, grad_expo = pl.pallas_call(
         scatter_kernel,
         out_shape=(pltpu.VMEM((own_count, G), F32), jax.ShapeDtypeStruct((1, 12), F32)),
-        in_specs=[smem(), vmem()],
+        in_specs=[vmem(), vmem()],
         out_specs=(vmem(), vmem()),
         name="scatter",
-    )(picks, near(returned))
+    )(near(picks), near(returned))
     sent_back = across(grad_proj, "view", views)
     grads = pl.pallas_call(
         unproject_kernel,
         out_shape=tuple(jax.ShapeDtypeStruct(piece.shape, F32) for piece in pieces),
-        in_specs=[vmem()] * 7,
+        in_specs=[vmem()] * 3,
         out_specs=tuple(vmem() for _ in pieces),
         name="unproject",
-    )(*pieces, cameras, near(sent_back))
+    )(near(kept), near(cams), near(sent_back))
     g_means, g_scales, g_rot, g_logits, g_coefs = grads
     return (
         shown.transpose(1, 0, 2)[None],

time: 134 us -> 130 us (0.970)
  Pallas kernels: 19.6 us -> 15.5 us
    pallas_call x1, Pallas kernels: 14 us -> 12.2 us  [render(): pl.pallas_call(render_kernel, out_shape=(jax.ShapeDtypeStruct((3, tiles,...]
where the time goes in v3:
time: 130 us
  blocking collectives  114 us (88%)
  Pallas kernels  15.5 us (12%)
    all_to_all x4, blocking collectives, across(): lax.all_to_all(shaped, axis, split_axis=0, concat_axis=0, tiled=True)  114 us
    pallas_call x1, Pallas kernels, render(): pl.pallas_call(render_kernel, out_shape=(jax.ShapeDtypeStruct((3, tiles,...  12.2 us

profile of v3, /device:TPU:1, one launch (start us, length us, event | category | flops | bytes accessed | tf_op | source)
XLA Modules:
  0.0 129.7 jit_solution(2245699600258586174)
XLA Ops:
  0.6 1.1 project.1
  1.7 14.1 %all_to_all.20 = f32[8,18,1,128]{3,2,1,0:T(1,128)S(1)} all-to-all(f32[8,18,1,128]{3,2,1,0:T(1,128)S(1)} %bitcast.31), channel_id=1, replica_groups=mesh['view'=8,'scene'=64] {'view'}, dimensions={0} | all-to-all | bytes 147456 | tf_op jit(solution)/shard_map/all_to_all | solution.py:544
  15.8 0.4 gather.1
  16.2 0.0 copy-start
  16.2 46.7 %all_to_all.21 = f32[64,18,1,128]{3,2,1,0:T(1,128)S(1)} all-to-all(f32[64,18,1,128]{3,2,1,0:T(1,128)S(1)} %bitcast.27), channel_id=1, replica_groups=mesh['view'=8,'scene'=64] {'scene'}, dimensions={0} | all-to-all | bytes 1179648 | tf_op jit(solution)/shard_map/all_to_all | solution.py:544
  62.9 0.0 copy-done
  62.9 12.2 %render.1 = (f32[3,16,256]{2,1,0:T(8,128)}, f32[1216,128]{1,0:T(8,128)S(1)}) custom-call(s32[16]{0:T(128)} %bitcast.38, s32[4,16]{1,0:T(4,128)} %bitcast.36, f32[1,12]{1,0:T(1,128)} %expo.1, f32[1152,128]{1,0:T(8,128)S(1)} %bitcast.26, f32[3,16,256]{2,1,0:T(8,128)S(1)} %bitcast.33), custom_call_target="tpu_custom_call" | custom-call | tf_op jit(solution)/shard_map/render/pallas_call | solution.py:558
  75.1 41.9 %all_to_all.22 = f32[64,19,1,128]{3,2,1,0:T(1,128)S(1)} all-to-all(f32[64,19,1,128]{3,2,1,0:T(1,128)S(1)} %bitcast.28), channel_id=1, replica_groups=mesh['view'=8,'scene'=64] {'scene'}, dimensions={0} | all-to-all | bytes 1245184 | tf_op jit(solution)/shard_map/all_to_all | solution.py:544
  117.0 0.7 scatter.1
  117.7 10.9 %all_to_all.23 = f32[8,18,1,128]{3,2,1,0:T(1,128)S(1)} all-to-all(f32[8,18,1,128]{3,2,1,0:T(1,128)S(1)} %bitcast.32), channel_id=1, replica_groups=mesh['view'=8,'scene'=64] {'view'}, dimensions={0} | all-to-all | bytes 147456 | tf_op jit(solution)/shard_map/all_to_all | solution.py:544
  128.6 1.1 unproject.1
Async XLA Ops:
  16.2 46.7 %copy-start = (f32[1,16,3,256]{3,1,2,0:T(8,128)S(1)}, f32[1,16,3,256]{3,1,2,0:T(8,128)}, u32[]{:S(2)}) copy-start(f32[1,16,3,256]{3,1,2,0:T(8,128)} %param.18) | copy-start | bytes 147460

commit v4 on v3

--- a/solution.py
+++ b/solution.py
@@ -388,7 +388,7 @@
 
     count = kmax * G
 
-    batch = 8
+    batch = 16
 
     def forward(step, keeps):
         keeps = list(keeps)
@@ -414,11 +414,12 @@
                 rows = pl.ds((group * kmax + k) * G * PITCH + t, G, stride=PITCH)
                 weight = jnp.concatenate([weights[0][rows, :], weights[1][rows, :]], axis=1)
                 w_high, w_low = split2(weight)
-                wt_h[spot * G : (spot + 1) * G, :] = w_high
-                wt_l[spot * G : (spot + 1) * G, :] = w_low
+                kept = ((group * 8 + t) * kmax + k) * G
+                wt_h[kept : kept + G, :] = w_high
+                wt_l[kept : kept + G, :] = w_low
                 own = mat_b[spot * 16 : (spot + 1) * 16, :]
-                total = total + dot(own, wt_h[spot * G : (spot + 1) * G, :])
-                total = total + dot(own, wt_l[spot * G : (spot + 1) * G, :])
+                total = total + dot(own, wt_h[kept : kept + G, :])
+                total = total + dot(own, wt_l[kept : kept + G, :])
             for channel in range(3):
                 row = channel * tiles + group * 8 + t
                 ccol[row : row + 1, :] = total[channel : channel + 1, :] + total[3 + channel : 4 + channel, :]
@@ -469,34 +470,43 @@
     def backward(step, behind):
         behind = list(behind)
         base = (count - batch - step * batch) * PITCH
+        gaps = [None] * (2 * groups)
         for inner in range(batch - 1, -1, -1):
             for group in range(groups):
                 rows = pl.ds(base + (group * count + inner) * PITCH, 8)
+                ahead = pl.ds(base + (group * count + max(inner - 1, 0)) * PITCH, 8)
                 for half in range(2):
                     at = group * 2 + half
-                    alpha = alphas[half][rows, :]
-                    value = slopes[half][rows, :]
-                    moved[half][rows, :] = weights[half][rows, :] * (value - behind[at])
-                    behind[at] = behind[at] * (1.0 - alpha) + alpha * value
+                    gap = slopes[half][rows, :] - behind[at] if gaps[at] is None else gaps[at]
+                    moved[half][rows, :] = weights[half][rows, :] * gap
+                    step_up = alphas[half][rows, :] * gap
+                    gaps[at] = (slopes[half][ahead, :] - behind[at]) - step_up
+                    behind[at] = behind[at] + step_up
         return tuple(behind)
 
     zeros = jnp.zeros((8, G), F32)
     lax.fori_loop(0, count // batch, backward, (zeros,) * (2 * groups))
 
+    pair = 2
     for group in range(groups):
-        for k in range(kmax):
-            for t in range(8):
-                spot = place(group, k, t)
-                rows = pl.ds((group * kmax + k) * G * PITCH + t, G, stride=PITCH)
-                value = jnp.concatenate([moved[0][rows, :].T, moved[1][rows, :].T], axis=0)
-                v_high, v_low = split2(value)
+        for t in range(8):
+            own = g_own[(group * 8 + t) * 16 : (group * 8 + t + 1) * 16, :]
+            for k0 in range(0, kmax, pair):
+                span = pair * G
+                values = []
+                for k in range(k0, k0 + pair):
+                    rows = pl.ds((group * kmax + k) * G * PITCH + t, G, stride=PITCH)
+                    values.append(jnp.concatenate([moved[0][rows, :].T, moved[1][rows, :].T], axis=0))
+                v_high, v_low = split2(jnp.concatenate(values, axis=1))
                 table = mono_t[...]
                 sums = dot(table, v_high) + dot(table, v_low)
-                mom[spot * PITCH : spot * PITCH + 8, :] = sums[0:8]
-                own = g_own[(group * 8 + t) * 16 : (group * 8 + t + 1) * 16, :]
-                w_high = wt_h[spot * G : (spot + 1) * G, :]
-                w_low = wt_l[spot * G : (spot + 1) * G, :]
-                mat_c[spot * 16 : (spot + 1) * 16, :] = dot_t(own, w_high) + dot_t(own, w_low)
+                kept = ((group * 8 + t) * kmax + k0) * G
+                tints = dot_t(own, wt_h[kept : kept + span, :]) + dot_t(own, wt_l[kept : kept + span, :])
+                for k in range(k0, k0 + pair):
+                    spot = place(group, k, t)
+                    side = slice((k - k0) * G, (k - k0 + 1) * G)
+                    mom[spot * PITCH : spot * PITCH + 8, :] = sums[0:8, side]
+                    mat_c[spot * 16 : (spot + 1) * 16, :] = tints[:, side]
 
     sum_0, sum_x, sum_y, sum_xx, sum_xy, sum_yy = [mom[pl.ds(i, picks, stride=PITCH), :] for i in range(6)]
     off_x, off_y, con_a, con_b, con_c, opac = [feature(i) for i in range(6)]

time: 130 us -> 130 us (level)
  no operation moved by 1% of the time
where the time goes in v4:
time: 130 us
  blocking collectives  114 us (88%)
  Pallas kernels  15.3 us (12%)
    all_to_all x4, blocking collectives, across(): lax.all_to_all(shaped, axis, split_axis=0, concat_axis=0, tiled=True)  114 us
    pallas_call x1, Pallas kernels, render(): pl.pallas_call(render_kernel, out_shape=(jax.ShapeDtypeStruct((3, tiles,...  12 us

profile of v4, /device:TPU:1, one launch (start us, length us, event | category | flops | bytes accessed | tf_op | source)
XLA Modules:
  0.0 129.5 jit_solution(14332338064104799169)
XLA Ops:
  0.6 1.1 project.1
  1.7 14.1 %all_to_all.20 = f32[8,18,1,128]{3,2,1,0:T(1,128)S(1)} all-to-all(f32[8,18,1,128]{3,2,1,0:T(1,128)S(1)} %bitcast.31), channel_id=1, replica_groups=mesh['view'=8,'scene'=64] {'view'}, dimensions={0} | all-to-all | bytes 147456 | tf_op jit(solution)/shard_map/all_to_all | solution.py:554
  15.8 0.4 gather.1
  16.2 0.0 copy-start
  16.2 46.7 %all_to_all.21 = f32[64,18,1,128]{3,2,1,0:T(1,128)S(1)} all-to-all(f32[64,18,1,128]{3,2,1,0:T(1,128)S(1)} %bitcast.27), channel_id=1, replica_groups=mesh['view'=8,'scene'=64] {'scene'}, dimensions={0} | all-to-all | bytes 1179648 | tf_op jit(solution)/shard_map/all_to_all | solution.py:554
  62.9 0.0 copy-done
  62.9 12.0 %render.1 = (f32[3,16,256]{2,1,0:T(8,128)}, f32[1216,128]{1,0:T(8,128)S(1)}) custom-call(s32[16]{0:T(128)} %bitcast.38, s32[4,16]{1,0:T(4,128)} %bitcast.36, f32[1,12]{1,0:T(1,128)} %expo.1, f32[1152,128]{1,0:T(8,128)S(1)} %bitcast.26, f32[3,16,256]{2,1,0:T(8,128)S(1)} %bitcast.33), custom_call_target="tpu_custom_call" | custom-call | tf_op jit(solution)/shard_map/render/pallas_call | solution.py:568
  74.9 41.9 %all_to_all.22 = f32[64,19,1,128]{3,2,1,0:T(1,128)S(1)} all-to-all(f32[64,19,1,128]{3,2,1,0:T(1,128)S(1)} %bitcast.28), channel_id=1, replica_groups=mesh['view'=8,'scene'=64] {'scene'}, dimensions={0} | all-to-all | bytes 1245184 | tf_op jit(solution)/shard_map/all_to_all | solution.py:554
  116.7 0.7 scatter.1
  117.5 11.0 %all_to_all.23 = f32[8,18,1,128]{3,2,1,0:T(1,128)S(1)} all-to-all(f32[8,18,1,128]{3,2,1,0:T(1,128)S(1)} %bitcast.32), channel_id=1, replica_groups=mesh['view'=8,'scene'=64] {'view'}, dimensions={0} | all-to-all | bytes 147456 | tf_op jit(solution)/shard_map/all_to_all | solution.py:554
  128.4 1.1 unproject.1
Async XLA Ops:
  16.2 46.7 %copy-start = (f32[1,16,3,256]{3,1,2,0:T(8,128)S(1)}, f32[1,16,3,256]{3,1,2,0:T(8,128)}, u32[]{:S(2)}) copy-start(f32[1,16,3,256]{3,1,2,0:T(8,128)} %param.18) | copy-start | bytes 147460

commit v5 on v4

--- a/solution.py
+++ b/solution.py
@@ -388,7 +388,7 @@
 
     count = kmax * G
 
-    batch = 16
+    batch = 32
 
     def forward(step, keeps):
         keeps = list(keeps)

time: 130 us -> 130 us (level)
  no operation moved by 1% of the time
where the time goes in v5:
time: 130 us; the launch traced here: 129 us
  blocking collectives  114 us (88%)
  Pallas kernels  15.1 us (12%)
    all_to_all x4, blocking collectives, across(): lax.all_to_all(shaped, axis, split_axis=0, concat_axis=0, tiled=True)  114 us
    pallas_call x1, Pallas kernels, render(): pl.pallas_call(render_kernel, out_shape=(jax.ShapeDtypeStruct((3, tiles,...  11.7 us

profile of v5, /device:TPU:1, one launch (start us, length us, event | category | flops | bytes accessed | tf_op | source)
XLA Modules:
  0.0 129.3 jit_solution(2955951293259865485)
XLA Ops:
  0.6 1.1 project.1
  1.7 14.1 %all_to_all.20 = f32[8,18,1,128]{3,2,1,0:T(1,128)S(1)} all-to-all(f32[8,18,1,128]{3,2,1,0:T(1,128)S(1)} %bitcast.31), channel_id=1, replica_groups=mesh['view'=8,'scene'=64] {'view'}, dimensions={0} | all-to-all | bytes 147456 | tf_op jit(solution)/shard_map/all_to_all | solution.py:554
  15.8 0.4 gather.1
  16.2 0.0 copy-start
  16.2 46.7 %all_to_all.21 = f32[64,18,1,128]{3,2,1,0:T(1,128)S(1)} all-to-all(f32[64,18,1,128]{3,2,1,0:T(1,128)S(1)} %bitcast.27), channel_id=1, replica_groups=mesh['view'=8,'scene'=64] {'scene'}, dimensions={0} | all-to-all | bytes 1179648 | tf_op jit(solution)/shard_map/all_to_all | solution.py:554
  62.9 0.0 copy-done
  62.9 11.7 %render.1 = (f32[3,16,256]{2,1,0:T(8,128)}, f32[1216,128]{1,0:T(8,128)S(1)}) custom-call(s32[16]{0:T(128)} %bitcast.38, s32[4,16]{1,0:T(4,128)} %bitcast.36, f32[1,12]{1,0:T(1,128)} %expo.1, f32[1152,128]{1,0:T(8,128)S(1)} %bitcast.26, f32[3,16,256]{2,1,0:T(8,128)S(1)} %bitcast.33), custom_call_target="tpu_custom_call" | custom-call | tf_op jit(solution)/shard_map/render/pallas_call | solution.py:568
  74.6 41.9 %all_to_all.22 = f32[64,19,1,128]{3,2,1,0:T(1,128)S(1)} all-to-all(f32[64,19,1,128]{3,2,1,0:T(1,128)S(1)} %bitcast.28), channel_id=1, replica_groups=mesh['view'=8,'scene'=64] {'scene'}, dimensions={0} | all-to-all | bytes 1245184 | tf_op jit(solution)/shard_map/all_to_all | solution.py:554
  116.5 0.7 scatter.1
  117.3 11.0 %all_to_all.23 = f32[8,18,1,128]{3,2,1,0:T(1,128)S(1)} all-to-all(f32[8,18,1,128]{3,2,1,0:T(1,128)S(1)} %bitcast.32), channel_id=1, replica_groups=mesh['view'=8,'scene'=64] {'view'}, dimensions={0} | all-to-all | bytes 147456 | tf_op jit(solution)/shard_map/all_to_all | solution.py:554
  128.2 1.1 unproject.1
Async XLA Ops:
  16.2 46.7 %copy-start = (f32[1,16,3,256]{3,1,2,0:T(8,128)S(1)}, f32[1,16,3,256]{3,1,2,0:T(8,128)}, u32[]{:S(2)}) copy-start(f32[1,16,3,256]{3,1,2,0:T(8,128)} %param.18) | copy-start | bytes 147460
